TPU v7x, 512 devices: a whole 4x4x16 slice. The times are simulated.
512 devices in a mesh: lon: 16 (over z), lat: 8 (over x, y_lo), ens: 4 (over y_hi, core).
Axes of the slice: x: 4, y: 4 (y_hi: 2, y_lo: 2; y = y_hi * 2 + y_lo), z: 16, core: 2. Of those that a mesh axis runs over, the one named last changes fastest.
Arguments:
- field: bfloat16 [4, 128, 1024, 128], P('ens', 'lat', 'lon'), may hold values from -6 to 6
- cotangent: bfloat16 [4, 128, 1024, 128], P('ens', 'lat', 'lon'), may hold values from -6 to 6
- land_mask: int32 [128, 1024], P('lat', 'lon'), may hold values from 0 to 1, as said below
- kernel_taps: float32 [49, 128], replicated, may hold values from -0.875 to 0.875
- norm_gain: float32 [128], replicated, may hold values from 0.1 to 1.9
- norm_shift: float32 [128], replicated, may hold values from -3 to 3
- up_weight: bfloat16 [128, 256], replicated, may hold values from -0.5 to 0.5
- down_weight: bfloat16 [256, 128], replicated, may hold values from -0.375 to 0.375
Outputs:
- output: bfloat16 [4, 128, 1024, 128], P('ens', 'lat', 'lon')
- field_grad: bfloat16 [4, 128, 1024, 128], P('ens', 'lat', 'lon')
- kernel_grad: float32 [49, 128], replicated
- norm_grad: float32 [2, 128], replicated
- up_grad: float32 [128, 256], replicated
- down_grad: float32 [256, 128], replicated
Inputs may be any that keep to these rules, and one draw needn't show every extreme that they name: `land_mask`: 1 marks an ocean cell and 0 a land cell; the share of ocean differs from tile to tile.
All inputs are finite; a program needn't handle non-finite values.
Results may differ from a plain program's by a relative error of at most 0.0062.
Values may be sent and summed in bfloat16 or wider, within the bound.
A program may use at most 64 MiB of HBM per device.

v0:
```python
import math

import jax
import jax.numpy as jnp
from jax import lax
from jax.sharding import PartitionSpec as P

KERNEL = 7
DILATION = 2
REACH = 6


def partner(shard, axis, bit):
    return lax.ppermute(shard, axis, [(i, i ^ 1 << bit) for i in range(lax.axis_size(axis))])


def extended_2(cells, sides, width, closed):
    for axis, dim in sides:
        count = lax.axis_size(axis)
        ends = count if closed else count - 1
        head = lax.slice_in_dim(cells, 0, width, axis=dim)
        tail = lax.slice_in_dim(cells, cells.shape[dim] - width, cells.shape[dim], axis=dim)
        cells = jnp.concatenate(
            [
                lax.ppermute(tail, axis, [(i, (i + 1) % count) for i in range(ends)]),
                cells,
                lax.ppermute(head, axis, [((i + 1) % count, i) for i in range(ends)]),
            ],
            axis=dim,
        )
    return cells


def shifted(block, axis, distance):
    devices = range(lax.axis_size(axis))
    route = [((i - distance) % len(devices), i) for i in devices]
    return lax.ppermute(block, axis, route)


def passed_along(value, axis, steps):
    count = lax.axis_size(axis)
    leading, last = (max(0, -steps), min(count, count - steps))
    return lax.ppermute(value, axis, [(source, source + steps) for source in range(leading, last)])


def depthwise(widened, kernel_taps, rows, cols):
    total = jnp.zeros((rows, cols, widened.shape[2]), jnp.float32)
    for row_tap in range(KERNEL):
        for col_tap in range(KERNEL):
            window = widened[
                DILATION * row_tap : DILATION * row_tap + rows,
                DILATION * col_tap : DILATION * col_tap + cols,
            ]
            total = total + kernel_taps[row_tap * KERNEL + col_tap] * window
    return total


def fold_forward(strip):
    for bit_pos in range(lax.axis_size("lon").bit_length() - 1):
        strip = partner(strip, "lon", bit_pos)
    return strip


def fold_backward(strip):
    for bit_pos in range(lax.axis_size("lon").bit_length() - 1):
        strip = partner(strip.astype(jnp.bfloat16), "lon", bit_pos).astype(strip.dtype)
    return strip


def is_northern():
    return lax.axis_index("lat") == lax.axis_size("lat") - 1


def extend_rows(block):
    padded = extended_2(block, (("lat", 0),), REACH, False)
    height = block.shape[0]
    folded = fold_forward(block[height - REACH :][::-1, ::-1])
    upper = jnp.where(is_northern(), folded, padded[height + REACH :])
    return jnp.concatenate([padded[: height + REACH], upper], 0)


def extend_cols(block):
    return extended_2(block, (("lon", 1),), REACH, True)


def retract_cols(grads):
    width = grads.shape[1] - 2 * REACH
    own = grads[:, REACH : REACH + width]
    from_east = shifted(grads[:, :REACH].astype(jnp.bfloat16), "lon", -1).astype(jnp.float32)
    from_west = shifted(grads[:, REACH + width :].astype(jnp.bfloat16), "lon", 1).astype(
        jnp.float32
    )
    own = own.at[:, width - REACH :].add(from_east)
    return own.at[:, :REACH].add(from_west)


def retract_rows(grads):
    height = grads.shape[0] - 2 * REACH
    own = grads[REACH : REACH + height]
    upper = grads[REACH + height :]
    from_north = passed_along(grads[:REACH].astype(jnp.bfloat16), "lat", -1).astype(jnp.float32)
    from_south = passed_along(upper.astype(jnp.bfloat16), "lat", 1).astype(upper.dtype)
    folded = fold_backward(upper[::-1, ::-1])
    own = own.at[height - REACH :].add(from_north + jnp.where(is_northern(), folded, 0.0))
    return own.at[:REACH].add(from_south)


def shards(field, cotangent, land_mask, kernel_taps, norm_gain, norm_shift, up_weight, down_weight):
    state = field[0]
    upstream_in = cotangent[0]
    rows, cols, channels = state.shape
    sea = land_mask.astype(jnp.float32)[:, :, None]
    masked = (state.astype(jnp.float32) * sea).astype(jnp.bfloat16)
    extended = extend_cols(extend_rows(masked))
    widened = extended.astype(jnp.float32)
    mixed = depthwise(widened, kernel_taps, rows, cols)
    centered = mixed - jnp.mean(mixed, -1, keepdims=True)
    rstd = lax.rsqrt(jnp.mean(centered * centered, -1, keepdims=True) + 1e-06)
    unit = centered * rstd
    normed = (unit * norm_gain + norm_shift).astype(jnp.bfloat16)
    cells = rows * cols
    flat_norm = normed.reshape(cells, channels)
    pre = jnp.dot(flat_norm, up_weight, preferred_element_type=jnp.float32)
    slope = math.sqrt(2.0 / math.pi)
    tanh_val = jnp.tanh(slope * (pre + 0.044715 * pre * pre * pre))
    activated = (0.5 * pre * (1.0 + tanh_val)).astype(jnp.bfloat16)
    product = jnp.dot(activated, down_weight, preferred_element_type=jnp.float32).reshape(
        rows, cols, channels
    )
    output = ((state.astype(jnp.float32) + product) * sea).astype(jnp.bfloat16)
    upstream = (upstream_in.astype(jnp.float32) * sea).astype(jnp.bfloat16)
    flat_up = upstream.reshape(cells, channels)
    down_part = jnp.dot(activated.T, flat_up, preferred_element_type=jnp.float32)
    act_grad = jnp.dot(flat_up, down_weight.T, preferred_element_type=jnp.float32)
    deriv = 0.5 * (1.0 + tanh_val) + 0.5 * pre * (1.0 - tanh_val * tanh_val) * slope * (
        1.0 + 3.0 * 0.044715 * pre * pre
    )
    pre_grad = (act_grad * deriv).astype(jnp.bfloat16)
    up_part = jnp.dot(flat_norm.T, pre_grad, preferred_element_type=jnp.float32)
    norm_in_grad = jnp.dot(pre_grad, up_weight.T, preferred_element_type=jnp.float32).reshape(
        rows, cols, channels
    )
    norm_part = jnp.stack([jnp.sum(norm_in_grad * unit, (0, 1)), jnp.sum(norm_in_grad, (0, 1))])
    count = cells * lax.axis_size("lon") * lax.axis_size("lat") * lax.axis_size("ens")
    factor = 1.0 / math.sqrt(count)
    scaled = norm_in_grad * norm_gain
    mixed_grad = rstd * (
        scaled
        - jnp.mean(scaled, -1, keepdims=True)
        - unit * jnp.mean(scaled * unit, -1, keepdims=True)
    )
    kernel_rows = []
    for row_tap in range(KERNEL):
        for col_tap in range(KERNEL):
            window = widened[
                DILATION * row_tap : DILATION * row_tap + rows,
                DILATION * col_tap : DILATION * col_tap + cols,
            ]
            kernel_rows.append(jnp.sum(window * mixed_grad, (0, 1)))
    kernel_part = jnp.stack(kernel_rows)
    margin = 2 * REACH
    spread_grad = jnp.pad(mixed_grad, ((margin, margin), (margin, margin), (0, 0)))
    extended_grad = jnp.zeros((rows + margin, cols + margin, channels), jnp.float32)
    for row_tap in range(KERNEL):
        for col_tap in range(KERNEL):
            row_start = margin - DILATION * row_tap
            col_start = margin - DILATION * col_tap
            window = spread_grad[
                row_start : row_start + rows + margin, col_start : col_start + cols + margin
            ]
            extended_grad = extended_grad + kernel_taps[row_tap * KERNEL + col_tap] * window
    masked_grad = retract_rows(retract_cols(extended_grad))
    field_grad = ((upstream_in.astype(jnp.float32) + masked_grad) * sea).astype(jnp.bfloat16)
    kernel_sum, norm_sum, up_sum, down_sum = lax.psum(
        (kernel_part, norm_part, up_part, down_part), ("lon", "lat", "ens")
    )
    return (
        output[None],
        field_grad[None],
        kernel_sum * factor,
        norm_sum * factor,
        up_sum * factor,
        down_sum * factor,
    )


def solution(mesh):
    in_specs = (
        P("ens", "lat", "lon", None),
        P("ens", "lat", "lon", None),
        P("lat", "lon"),
        P(),
        P(),
        P(),
        P(),
        P(),
    )
    out_specs = (P("ens", "lat", "lon", None), P("ens", "lat", "lon", None), P(), P(), P(), P())
    return jax.shard_map(shards, mesh=mesh, in_specs=in_specs, out_specs=out_specs, check_vma=False)
```

profile of v0, /device:TPU:1, one launch (start us, length us, event | category | flops | bytes accessed | tf_op | source)
XLA Modules:
  0.0 698.0 jit_solution(13167900297526407773)
XLA Ops:
  7.2 0.0 copy-start
  7.2 0.0 copy-start.2
  7.2 0.0 all-reduce.5.cloned.1.call-start
  7.3 0.8 convert_element_type.87
  8.0 1.1 fusion.106
  9.2 4.4 collective-permute-start.1
  13.6 3.2 collective-permute-start
  16.8 1.3 collective-permute-start.5
  18.1 0.1 mul.1350
  18.2 4.9 collective-permute-start.2
  23.1 0.2 fusion.107
  23.3 2.6 collective-permute-done.2
  25.9 11.0 %collective-permute-start.3 = (bf16[6,64,128]{2,1,0:T(8,128)(2,1)S(1)}, bf16[6,64,128]{2,1,0:T(8,128)(2,1)S(1)}, u32[]{:S(2)}, u32[]{:S(2)}) collective-permute-start(bf16[6,64,128]{2,1,0:T(8,128)(2,1)S(1)} %collective-permute-done.2), channel_id=1, source_target_pairs={{0,128},{32,160},{64,192},{96,224},{128,0},{160,32},{192,64},{224,... | collective-permute-start | bytes 294920 | tf_op jit(solution)/shard_map/ppermute | solution.py:14
  36.9 7.3 %collective-permute-done.3 = bf16[6,64,128]{2,1,0:T(8,128)(2,1)S(1)} collective-permute-done((bf16[6,64,128]{2,1,0:T(8,128)(2,1)S(1)}, bf16[6,64,128]{2,1,0:T(8,128)(2,1)S(1)}, u32[]{:S(2)}, u32[]{:S(2)}) %collective-permute-start.3) | collective-permute-done | bytes 98336 | tf_op jit(solution)/shard_map/ppermute | solution.py:14
  44.2 11.7 %collective-permute-start.4 = (bf16[6,64,128]{2,1,0:T(8,128)(2,1)S(1)}, bf16[6,64,128]{2,1,0:T(8,128)(2,1)S(1)}, u32[]{:S(2)}, u32[]{:S(2)}) collective-permute-start(bf16[6,64,128]{2,1,0:T(8,128)(2,1)S(1)} %collective-permute-done.3), channel_id=1, source_target_pairs={{0,256},{32,288},{64,320},{96,352},{128,384},{160,416},{192,448},{... | collective-permute-start | bytes 294920 | tf_op jit(solution)/shard_map/ppermute | solution.py:14
  56.0 0.0 collective-permute-done.5
  56.0 2.5 collective-permute-done.4
  58.5 0.0 collective-permute-done
  58.5 1.9 collective-permute-start.6
  60.4 7.2 %collective-permute-start.7 = (bf16[28,6,128]{2,1,0:T(8,128)(2,1)S(1)}, bf16[28,6,128]{2,1,0:T(8,128)(2,1)S(1)}, u32[]{:S(2)}, u32[]{:S(2)}) collective-permute-start(bf16[28,6,128]{2,1,0:T(8,128)(2,1)S(1)} %get-tuple-element.122), channel_id=1, source_target_pairs={{32,0},{64,32},{96,64},{128,96},{160,128},{192,160},{224,192},{256... | collective-permute-start | bytes 129032 | tf_op jit(solution)/shard_map/ppermute | solution.py:27
  67.7 1.2 collective-permute-done.7
  68.9 0.2 maximum_convert_fusion
  69.1 0.0 copy-start.6
  69.1 0.0 copy-start.7
  69.1 3.9 fusion.116
  73.1 0.4 multiply_reduce_fusion.52
  73.5 0.3 add_convert_fusion
  73.9 0.0 copy-start.4
  73.9 0.5 multiply_convert_fusion
  74.4 1.0 fusion.122
  75.4 0.3 fusion.120
  75.7 0.8 fusion
  76.4 0.9 fusion.121
  77.4 0.4 fusion.113
  77.8 0.1 div.17
  77.8 0.5 multiply_reduce_fusion
  78.4 1.5 multiply_reduce_fusion.1
  79.9 0.7 multiply_reduce_fusion.37
  80.5 0.9 multiply_reduce_fusion.19
  81.4 10.4 %fusion.114 = (bf16[28,76,128]{2,1,0:T(8,128)(2,1)S(1)}, f32[28,76,128]{2,1,0:T(8,128)S(1)}) fusion(f32[128]{0:T(128)S(1)} %get-tuple-element.172, f32[128]{0:T(128)S(1)} %get-tuple-element.173, f32[128]{0:T(128)S(1)} %get-tuple-element.126, f32[128]{0:T(128)S(1)} %get-tuple-element.127, f32[128]{0:T(128)S(1)} %get-tuple-element.128, ...), kind=kLoop, calls=%fused_computation.297 | loop fusion | flops 26693632 | bytes 2183680 | tf_op jit(solution)/shard_map/convert.5
  91.9 0.9 fusion.104
  92.8 1.9 collective-permute-start.9
  94.8 5.1 collective-permute-start.8
  99.9 0.1 slice.883
  100.0 0.1 stack.208
  100.1 105.6 %all-reduce.1 = (f32[49,128]{1,0:T(8,128)S(1)}, f32[2,128]{1,0:T(2,128)S(1)}) all-reduce(f32[49,128]{1,0:T(8,128)S(1)} %stack.208, f32[2,128]{1,0:T(2,128)S(1)} %pad_maximum_fusion.3), channel_id=1, replica_groups=mesh['lon'=16,'lat'=8,'ens'=4] {'lon','lat','ens'}, use_global_device_ids=true, to_apply=%region_53.54 | all-reduce | flops 6528 | bytes 52224 | tf_op jit(solution)/shard_map/psum | solution.py:174
  205.8 0.2 scatter-add.14
  206.0 0.0 collective-permute-done.9
  206.0 0.2 scatter-add.15
  206.3 2.8 collective-permute-start.11
  209.2 0.6 broadcast_multiply_fusion.2
  209.8 0.0 all-reduce.5.cloned.1.call-update
  209.8 1.9 collective-permute-done.11
  211.7 3.2 collective-permute-start.12
  214.9 0.6 broadcast_multiply_fusion.6
  215.5 2.2 collective-permute-start.15
  217.7 1.3 collective-permute-start.10
  219.1 6.2 collective-permute-start.13
  225.3 445.4 %all-reduce.5.cloned.1.call-done = (f32[128,256]{1,0:T(8,128)}, f32[256,128]{1,0:T(8,128)}) async-done(((f32[128,256]{1,0:T(8,128)}, f32[256,128]{1,0:T(8,128)}), (f32[128,256]{1,0:T(8,128)}, f32[256,128]{1,0:T(8,128)})) %all-reduce.5.cloned.1.call-update) | async-done | bytes 262160 | tf_op jit(solution)/shard_map/psum | solution.py:174
  670.7 1.6 broadcast_multiply_fusion.1
  672.3 9.8 %collective-permute-start.14 = (bf16[6,64,128]{2,1,0:T(8,128)(2,1)S(1)}, bf16[6,64,128]{2,1,0:T(8,128)(2,1)S(1)}, u32[]{:S(2)}, u32[]{:S(2)}) collective-permute-start(bf16[6,64,128]{2,1,0:T(8,128)(2,1)S(1)} %collective-permute-done.13), channel_id=1, source_target_pairs={{0,256},{32,288},{64,320},{96,352},{128,384},{160,416},{192,448},{... | collective-permute-start | bytes 294920 | tf_op jit(solution)/shard_map/ppermute | solution.py:14
  682.1 1.6 broadcast_multiply_fusion
  683.6 6.5 collective-permute-done.14
  690.2 0.9 fusion.110
  (38 shorter events, 0.5 us)
Async XLA Ops:
  7.2 66.7 %copy-start = (bf16[128,256]{1,0:T(8,128)(2,1)S(1)}, bf16[128,256]{1,0:T(8,128)(2,1)}, u32[]{:S(2)}) copy-start(bf16[128,256]{1,0:T(8,128)(2,1)} %param.22) | copy-start | bytes 196612
  7.2 15.9 %copy-start.2 = (bf16[1,16,64,128]{3,2,1,0:T(8,128)(2,1)S(1)}, bf16[1,16,64,128]{3,2,1,0:T(8,128)(2,1)}, u32[]{:S(2)}) copy-start(bf16[1,16,64,128]{3,2,1,0:T(8,128)(2,1)} %param.17) | copy-start | bytes 786436
  7.2 29.7 %copy-start.5 = (f32[49,128]{1,0:T(8,128)S(1)}, f32[49,128]{1,0:T(8,128)}, u32[]{:S(2)}) copy-start(f32[49,128]{1,0:T(8,128)} %param.19) | copy-start | bytes 75268
  7.2 663.5 %all-reduce.5.cloned.1.call-start = ((), (), s32[]{:S(2)}) async-start(), calls=%async_computation | async-start | bytes 524288 | tf_op jit(solution)/shard_map/psum | solution.py:174
  9.2 9.0 %collective-permute-start.1 = (bf16[6,64,128]{2,1,0:T(8,128)(2,1)S(1)}, bf16[6,64,128]{2,1,0:T(8,128)(2,1)S(1)}, u32[]{:S(2)}, u32[]{:S(2)}) collective-permute-start(bf16[6,64,128]{2,1,0:T(8,128)(2,1)S(1)} %rev.6), channel_id=1, source_target_pairs={{0,32},{32,0},{64,96},{96,64},{128,160},{160,128},{192,224},{224,1... | collective-permute-start | bytes 294920 | tf_op jit(solution)/shard_map/ppermute | solution.py:14
  13.6 44.9 %collective-permute-start = (bf16[6,64,128]{2,1,0:T(8,128)(2,1)S(1)}, bf16[6,64,128]{2,1,0:T(8,128)(2,1)S(1)}, u32[]{:S(2)}, u32[]{:S(2)}) collective-permute-start(bf16[6,64,128]{2,1,0:T(8,128)(2,1)S(1)} %get-tuple-element.124), channel_id=1, source_target_pairs={{0,4},{4,8},{8,12},{12,16},{16,20},{20,24},{24,28},{1,5},{5,9},{9,... | collective-permute-start | bytes 294920 | tf_op jit(solution)/shard_map/ppermute | solution.py:25
  16.8 39.1 %collective-permute-start.5 = (bf16[6,64,128]{2,1,0:T(8,128)(2,1)S(1)}, bf16[6,64,128]{2,1,0:T(8,128)(2,1)S(1)}, u32[]{:S(2)}, u32[]{:S(2)}) collective-permute-start(bf16[6,64,128]{2,1,0:T(8,128)(2,1)S(1)} %get-tuple-element.123), channel_id=1, source_target_pairs={{4,0},{8,4},{12,8},{16,12},{20,16},{24,20},{28,24},{5,1},{9,5},{13... | collective-permute-start | bytes 294920 | tf_op jit(solution)/shard_map/ppermute | solution.py:27
  18.2 7.7 %collective-permute-start.2 = (bf16[6,64,128]{2,1,0:T(8,128)(2,1)S(1)}, bf16[6,64,128]{2,1,0:T(8,128)(2,1)S(1)}, u32[]{:S(2)}, u32[]{:S(2)}) collective-permute-start(bf16[6,64,128]{2,1,0:T(8,128)(2,1)S(1)} %collective-permute-done.1), channel_id=1, source_target_pairs={{0,64},{32,96},{64,0},{96,32},{128,192},{160,224},{192,128},{224,1... | collective-permute-start | bytes 294920 | tf_op jit(solution)/shard_map/ppermute | solution.py:14
  25.9 18.3 %collective-permute-start.3 = (bf16[6,64,128]{2,1,0:T(8,128)(2,1)S(1)}, bf16[6,64,128]{2,1,0:T(8,128)(2,1)S(1)}, u32[]{:S(2)}, u32[]{:S(2)}) collective-permute-start(bf16[6,64,128]{2,1,0:T(8,128)(2,1)S(1)} %collective-permute-done.2), channel_id=1, source_target_pairs={{0,128},{32,160},{64,192},{96,224},{128,0},{160,32},{192,64},{224,... | collective-permute-start | bytes 294920 | tf_op jit(solution)/shard_map/ppermute | solution.py:14
  44.2 14.3 %collective-permute-start.4 = (bf16[6,64,128]{2,1,0:T(8,128)(2,1)S(1)}, bf16[6,64,128]{2,1,0:T(8,128)(2,1)S(1)}, u32[]{:S(2)}, u32[]{:S(2)}) collective-permute-start(bf16[6,64,128]{2,1,0:T(8,128)(2,1)S(1)} %collective-permute-done.3), channel_id=1, source_target_pairs={{0,256},{32,288},{64,320},{96,352},{128,384},{160,416},{192,448},{... | collective-permute-start | bytes 294920 | tf_op jit(solution)/shard_map/ppermute | solution.py:14
  58.5 9.2 %collective-permute-start.6 = (bf16[28,6,128]{2,1,0:T(8,128)(2,1)S(1)}, bf16[28,6,128]{2,1,0:T(8,128)(2,1)S(1)}, u32[]{:S(2)}, u32[]{:S(2)}) collective-permute-start(bf16[28,6,128]{2,1,0:T(8,128)(2,1)S(1)} %get-tuple-element.121), channel_id=1, source_target_pairs={{0,32},{32,64},{64,96},{96,128},{128,160},{160,192},{192,224},{224... | collective-permute-start | bytes 129032 | tf_op jit(solution)/shard_map/ppermute | solution.py:25
  60.4 8.5 %collective-permute-start.7 = (bf16[28,6,128]{2,1,0:T(8,128)(2,1)S(1)}, bf16[28,6,128]{2,1,0:T(8,128)(2,1)S(1)}, u32[]{:S(2)}, u32[]{:S(2)}) collective-permute-start(bf16[28,6,128]{2,1,0:T(8,128)(2,1)S(1)} %get-tuple-element.122), channel_id=1, source_target_pairs={{32,0},{64,32},{96,64},{128,96},{160,128},{192,160},{224,192},{256... | collective-permute-start | bytes 129032 | tf_op jit(solution)/shard_map/ppermute | solution.py:27
  69.1 4.4 copy-start.6
  69.1 4.4 copy-start.7
  73.9 1.5 copy-start.4
  81.4 10.5 %copy-start.1 = (bf16[1,16,64,128]{3,2,1,0:T(8,128)(2,1)S(1)}, bf16[1,16,64,128]{3,2,1,0:T(8,128)(2,1)}, u32[]{:S(2)}) copy-start(bf16[1,16,64,128]{3,2,1,0:T(8,128)(2,1)} %param.16) | copy-start | bytes 786436
  92.8 113.2 %collective-permute-start.9 = (bf16[28,6,128]{2,1,0:T(8,128)(2,1)S(1)}, bf16[28,6,128]{2,1,0:T(8,128)(2,1)S(1)}, u32[]{:S(2)}, u32[]{:S(2)}) collective-permute-start(bf16[28,6,128]{2,1,0:T(8,128)(2,1)S(1)} %get-tuple-element.119), channel_id=1, source_target_pairs={{480,0},{0,32},{32,64},{64,96},{96,128},{128,160},{160,192},{192,2... | collective-permute-start | bytes 129032 | tf_op jit(solution)/shard_map/ppermute | solution.py:37
  94.8 111.0 %collective-permute-start.8 = (bf16[28,6,128]{2,1,0:T(8,128)(2,1)S(1)}, bf16[28,6,128]{2,1,0:T(8,128)(2,1)S(1)}, u32[]{:S(2)}, u32[]{:S(2)}) collective-permute-start(bf16[28,6,128]{2,1,0:T(8,128)(2,1)S(1)} %get-tuple-element.120), channel_id=1, source_target_pairs={{32,0},{64,32},{96,64},{128,96},{160,128},{192,160},{224,192},{256... | collective-permute-start | bytes 129032 | tf_op jit(solution)/shard_map/ppermute | solution.py:37
  206.3 5.4 collective-permute-start.11
  211.7 7.4 %collective-permute-start.12 = (bf16[6,64,128]{2,1,0:T(8,128)(2,1)S(1)}, bf16[6,64,128]{2,1,0:T(8,128)(2,1)S(1)}, u32[]{:S(2)}, u32[]{:S(2)}) collective-permute-start(bf16[6,64,128]{2,1,0:T(8,128)(2,1)S(1)} %collective-permute-done.11), channel_id=1, source_target_pairs={{0,64},{32,96},{64,0},{96,32},{128,192},{160,224},{192,128},{224,1... | collective-permute-start | bytes 294920 | tf_op jit(solution)/shard_map/ppermute | solution.py:14
  215.5 474.8 %copy-start.3 = (bf16[1,16,64,128]{3,2,1,0:T(8,128)(2,1)S(1)}, bf16[1,16,64,128]{3,2,1,0:T(8,128)(2,1)}, u32[]{:S(2)}) copy-start(bf16[1,16,64,128]{3,2,1,0:T(8,128)(2,1)} %param.17) | copy-start | bytes 786436
  215.5 474.7 %collective-permute-start.15 = (bf16[6,64,128]{2,1,0:T(8,128)(2,1)S(1)}, bf16[6,64,128]{2,1,0:T(8,128)(2,1)S(1)}, u32[]{:S(2)}, u32[]{:S(2)}) collective-permute-start(bf16[6,64,128]{2,1,0:T(8,128)(2,1)S(1)} %get-tuple-element.116), channel_id=1, source_target_pairs={{0,4},{4,8},{8,12},{12,16},{16,20},{20,24},{24,28},{1,5},{5,9},{9,... | collective-permute-start | bytes 294920 | tf_op jit(solution)/shard_map/ppermute | solution.py:43
  217.7 465.9 %collective-permute-start.10 = (bf16[6,64,128]{2,1,0:T(8,128)(2,1)S(1)}, bf16[6,64,128]{2,1,0:T(8,128)(2,1)S(1)}, u32[]{:S(2)}, u32[]{:S(2)}) collective-permute-start(bf16[6,64,128]{2,1,0:T(8,128)(2,1)S(1)} %get-tuple-element.118), channel_id=1, source_target_pairs={{4,0},{8,4},{12,8},{16,12},{20,16},{24,20},{28,24},{5,1},{9,5},{13... | collective-permute-start | bytes 294920 | tf_op jit(solution)/shard_map/ppermute | solution.py:43
  219.1 453.2 %collective-permute-start.13 = (bf16[6,64,128]{2,1,0:T(8,128)(2,1)S(1)}, bf16[6,64,128]{2,1,0:T(8,128)(2,1)S(1)}, u32[]{:S(2)}, u32[]{:S(2)}) collective-permute-start(bf16[6,64,128]{2,1,0:T(8,128)(2,1)S(1)} %collective-permute-done.12), channel_id=1, source_target_pairs={{0,128},{32,160},{64,192},{96,224},{128,0},{160,32},{192,64},{224,... | collective-permute-start | bytes 294920 | tf_op jit(solution)/shard_map/ppermute | solution.py:14
  672.3 17.9 %collective-permute-start.14 = (bf16[6,64,128]{2,1,0:T(8,128)(2,1)S(1)}, bf16[6,64,128]{2,1,0:T(8,128)(2,1)S(1)}, u32[]{:S(2)}, u32[]{:S(2)}) collective-permute-start(bf16[6,64,128]{2,1,0:T(8,128)(2,1)S(1)} %collective-permute-done.13), channel_id=1, source_target_pairs={{0,256},{32,288},{64,320},{96,352},{128,384},{160,416},{192,448},{... | collective-permute-start | bytes 294920 | tf_op jit(solution)/shard_map/ppermute | solution.py:14
Sparse Core Ops, SparseCore 0:
  209.9 460.6 all-reduce.4
where the time goes:
time: 699 us; the launch traced here: 698 us
  waiting for transfers between devices  467 us (67%)
  blocking collectives  106 us (15%)
  starting transfers between devices  78.3 us (11%)
  other arithmetic  27.3 us (4%)
  between operations  14.5 us (2%)
    psum x1, waiting for transfers between devices, shards(): lax.psum((kernel_part, norm_part, up_part, down_part), ('lon', 'lat', 'en...  445 us
    psum x1, blocking collectives, shards(): lax.psum((kernel_part, norm_part, up_part, down_part), ('lon', 'lat', 'en...  106 us
    ppermute x8, starting transfers between devices, partner(): lax.ppermute(shard, axis, [(i, i ^ 1 << bit) for i in range(lax.axis_size...  54.1 us
    ppermute x8, waiting for transfers between devices, partner(): lax.ppermute(shard, axis, [(i, i ^ 1 << bit) for i in range(lax.axis_size...  20.7 us
  transfers between devices with their start and end apart: 17, of which 7 were waited for; matrix products, arithmetic and copies ran while one was open for 1% of the time, Pallas kernels for 0%

commit v1 on v0

v1 whole, which is shorter than its diff:
```python
import functools
import math

import jax
import jax.numpy as jnp
from jax import lax
from jax.experimental import pallas as pl
from jax.experimental.pallas import tpu as pltpu
from jax.sharding import PartitionSpec as P

KERNEL = 7
REACH = 6
TAPS = KERNEL * KERNEL
MESH = pl.DeviceIdType.MESH
F32 = jnp.float32
BF16 = jnp.bfloat16
SLOPE = math.sqrt(2.0 / math.pi)
CUBIC = 0.044715

SOUTH, CENTER, NORTH = 0, 1, 2
WEST, MIDDLE, EAST = 0, 1, 2


def rdot(a, b):
    return lax.dot_general(a, b, (((1,), (1,)), ((), ())), preferred_element_type=F32)


def tdot(a, b):
    return lax.dot_general(a, b, (((0,), (0,)), ((), ())), preferred_element_type=F32)


def phases_of(blocks):
    count = blocks.shape[0]
    sub = lax.broadcasted_iota(jnp.int32, (count - 1, 8, 128), 1)
    out = []
    for shift in (2, 4, 6):
        rolled = pltpu.roll(blocks, 8 - shift, 1)
        out.append(jnp.where(sub < 8 - shift, rolled[: count - 1], rolled[1:]))
    return out


def region(ref, rows, cols):
    return ref.at[pl.ds(*rows), pl.ds(*cols)]


DST_ROWS = {SOUTH: (0, 6), CENTER: (6, 16), NORTH: (22, 6)}
DST_COLS = {WEST: (0, 1), MIDDLE: (1, 8), EAST: (9, 1)}
REGIONS = [(r, c) for r in range(3) for c in range(3) if (r, c) != (CENTER, MIDDLE)]


class Grid:
    def __init__(self, nlon, nlat, nens):
        self.nlon, self.nlat, self.nens = nlon, nlat, nens
        self.lon = lax.axis_index("lon")
        self.lat = lax.axis_index("lat")
        self.ens = lax.axis_index("ens")
        self.north = self.lat == nlat - 1
        self.plane = self.lat * nens + self.ens
        self.planes = nlat * nens


def halo_start(g, src, dst, src_rows, src_cols, ssem, rsem, only_rows):
    for rr, cc in REGIONS:
        if rr not in only_rows:
            continue
        here = region(src, src_rows[rr], src_cols[cc])
        land_c = 2 - cc
        step = cc - 1
        east = lax.rem(g.lon + step + g.nlon, g.nlon)

        def send(lat, lon, land_r, here=here, rr=rr, cc=cc, land_c=land_c):
            pltpu.make_async_remote_copy(
                src_ref=here,
                dst_ref=region(dst, DST_ROWS[land_r], DST_COLS[land_c]),
                send_sem=ssem.at[rr * 3 + cc],
                recv_sem=rsem.at[land_r * 3 + land_c],
                device_id={"lon": lon, "lat": lat},
                device_id_type=MESH,
            ).start()

        if rr == CENTER:
            send(g.lat, east, CENTER)
        elif rr == SOUTH:

            @pl.when(g.lat > 0)
            def _(send=send, east=east):
                send(g.lat - 1, east, NORTH)

        else:
            across = lax.rem(2 * g.nlon - 1 - g.lon - step, g.nlon)

            @pl.when(jnp.logical_not(g.north))
            def _(send=send, east=east):
                send(g.lat + 1, east, SOUTH)

            @pl.when(jnp.logical_and(g.north, across != g.lon))
            def _(send=send, across=across):
                send(g.lat, across, NORTH)

            if cc != MIDDLE:

                @pl.when(jnp.logical_and(g.north, across == g.lon))
                def _(here=here, land_c=land_c):
                    pltpu.make_async_copy(
                        here,
                        region(dst, DST_ROWS[NORTH], DST_COLS[land_c]),
                        rsem.at[NORTH * 3 + land_c],
                    ).start()


def halo_wait_recv(g, dst, rsem, row):
    for cc in range(3):
        if (row, cc) == (CENTER, MIDDLE):
            continue
        part = region(dst, DST_ROWS[row], DST_COLS[cc])
        wait = pltpu.make_async_copy(part, part, rsem.at[row * 3 + cc]).wait
        if row == SOUTH:
            pl.when(g.lat > 0)(wait)
        else:
            wait()


def halo_wait_send(g, src, src_rows, src_cols, ssem):
    for rr, cc in REGIONS:
        here = region(src, src_rows[rr], src_cols[cc])
        wait = pltpu.make_async_copy(here, here, ssem.at[rr * 3 + cc]).wait
        if rr == CENTER:
            wait()
        elif rr == SOUTH:
            pl.when(g.lat > 0)(wait)
        elif cc == MIDDLE:
            wait()
        else:
            across = lax.rem(2 * g.nlon - 1 - g.lon - (cc - 1), g.nlon)
            pl.when(jnp.logical_or(jnp.logical_not(g.north), across != g.lon))(wait)


def plane_send(g, src_of, dst, ssem, rsem):
    def one(k, carry):
        peer = lax.rem(g.plane + k, g.planes)
        pltpu.make_async_remote_copy(
            src_ref=src_of(peer),
            dst_ref=dst.at[g.plane],
            send_sem=ssem,
            recv_sem=rsem,
            device_id={"lat": peer // g.nens, "ens": lax.rem(peer, g.nens)},
            device_id_type=MESH,
        ).start()
        return carry

    lax.fori_loop(1, g.planes, one, 0)


def lon_send(g, buf, ssem, rsem):
    def one(k, carry):
        pltpu.make_async_remote_copy(
            src_ref=buf.at[g.lon],
            dst_ref=buf.at[g.lon],
            send_sem=ssem,
            recv_sem=rsem,
            device_id={"lon": lax.rem(g.lon + k, g.nlon)},
            device_id_type=MESH,
        ).start()
        return carry

    lax.fori_loop(1, g.nlon, one, 0)


def bulk_wait(buf, count, sem):
    part = buf.at[pl.ds(0, count)]
    pltpu.make_async_copy(part, part, sem).wait()


FWD_ROWS = {SOUTH: (6, 6), CENTER: (6, 16), NORTH: (16, 6)}
FWD_COLS = {WEST: (1, 1), MIDDLE: (1, 8), EAST: (8, 1)}
BWD_ROWS = {SOUTH: (0, 6), CENTER: (6, 16), NORTH: (22, 6)}
BWD_COLS = {WEST: (0, 1), MIDDLE: (1, 8), EAST: (9, 1)}


def kernel(
    sizes,
    field, cotangent, mask, taps, gain, shift, up, down,
    output, field_grad, kernel_grad, norm_grad, up_grad, down_grad,
    ext, sea, ep, kt, ups, mixed, normed, active, pregrad, nacc, mp, kacc, eg, egs, rb,
    pay1, ra1, zb1, gb1, pay2, ra2, zb2, gb2,
    fs, fr, bs, br, ar_s, ar_r,
):
    g = Grid(*sizes)
    factor = 1.0 / math.sqrt(1024 * g.nlon * g.nlat * g.nens)

    barrier = pltpu.get_barrier_semaphore()

    def greet(**where):
        pl.semaphore_signal(barrier, inc=1, device_id=where, device_id_type=MESH)

    def greet_plane(k, carry):
        peer = lax.rem(g.plane + k, g.planes)
        greet(lat=peer // g.nens, ens=lax.rem(peer, g.nens))
        return carry

    def greet_lon(k, carry):
        greet(lon=lax.rem(g.lon + k, g.nlon))
        return carry

    east = lax.rem(g.lon + 1, g.nlon)
    west = lax.rem(g.lon + g.nlon - 1, g.nlon)

    @pl.when(g.lat > 0)
    def _():
        greet(lat=g.lat - 1, lon=east)
        greet(lat=g.lat - 1, lon=west)

    @pl.when(g.lat < g.nlat - 1)
    def _():
        greet(lat=g.lat + 1, lon=east)
        greet(lat=g.lat + 1, lon=west)

    lax.fori_loop(1, g.planes, greet_plane, 0)
    lax.fori_loop(1, g.nlon, greet_lon, 0)

    eye = (
        lax.broadcasted_iota(jnp.int32, (64, 64), 0) == lax.broadcasted_iota(jnp.int32, (64, 64), 1)
    )
    ones = jnp.ones((64, 128), BF16)

    def mask_row(r, carry):
        marks = jnp.broadcast_to(mask[pl.ds(r, 1), :].astype(F32), (64, 64))
        spread = jnp.where(eye, marks, 0.0).astype(BF16)
        wide = jnp.dot(spread, ones, preferred_element_type=F32).reshape(8, 8, 128)
        sea[r] = wide
        ext[r + REACH, 1:9] = (field[r].astype(F32) * wide).astype(BF16)
        return carry

    lax.fori_loop(0, 16, mask_row, 0)

    count = g.planes + g.nlon - 2
    count = count + 2 * (g.lat > 0).astype(jnp.int32) + 2 * (g.lat < g.nlat - 1).astype(jnp.int32)
    pl.semaphore_wait(barrier, count)
    halo_start(g, ext, ext, FWD_ROWS, FWD_COLS, fs, fr, (NORTH, SOUTH, CENTER))

    def upstream_row(r, carry):
        wide = cotangent[r].astype(F32) * sea[r]
        ups[pl.ds(pl.multiple_of(r * 64, 64), 64), :] = wide.reshape(64, 128).astype(BF16)
        return carry

    lax.fori_loop(0, 16, upstream_row, 0)
    for t in range(TAPS):
        kt[t] = jnp.broadcast_to(taps[t : t + 1, :], (8, 128))
    nacc[...] = jnp.zeros_like(nacc)
    kacc[...] = jnp.zeros_like(kacc)

    def widen_row(r, carry):
        blocks = ext[r].astype(F32)
        ep[0, r] = blocks
        for k, moved in enumerate(phases_of(blocks)):
            ep[k + 1, r, 0:9] = moved
        return carry

    halo_wait_recv(g, ext, fr, CENTER)
    lax.fori_loop(REACH, 16 + REACH, widen_row, 0)

    halo_wait_recv(g, ext, fr, SOUTH)

    @pl.when(g.lat == 0)
    def _():
        ext[0:REACH] = jnp.zeros((REACH, 10, 8, 128), BF16)

    lax.fori_loop(0, REACH, widen_row, 0)

    def conv_row(r, carry):
        total = jnp.zeros((8, 8, 128), F32)
        for i in range(KERNEL):
            for j in range(KERNEL):
                off = 2 + 2 * j
                ph, skip = (off % 8) // 2, off // 8
                total = total + kt[i * KERNEL + j][None] * ep[ph, r + 2 * i, skip : skip + 8]
        mixed[pl.ds(pl.multiple_of(r * 64, 64), 64), :] = total.reshape(64, 128)
        return carry

    gain_row = gain[...]
    shift_row = shift[...]

    def group(q, carry):
        lax.fori_loop(4 * q, 4 * q + 4, conv_row, 0)
        cells = pl.ds(pl.multiple_of(q * 256, 256), 256)
        x = mixed[cells, :]
        centered = x - jnp.mean(x, -1, keepdims=True)
        rstd = lax.rsqrt(jnp.mean(centered * centered, -1, keepdims=True) + 1e-06)
        unit = centered * rstd
        norm = (unit * gain_row + shift_row).astype(BF16)
        normed[cells, :] = norm
        pre = jnp.dot(norm, up[...], preferred_element_type=F32)
        square = pre * pre
        tanh_val = jnp.tanh(SLOPE * (pre + CUBIC * pre * square))
        half = 0.5 * (1.0 + tanh_val)
        act = (pre * half).astype(BF16)
        active[cells, :] = act
        product = jnp.dot(act, down[...], preferred_element_type=F32).reshape(4, 8, 8, 128)
        rows = pl.ds(4 * q, 4)
        output[rows] = ((field[rows].astype(F32) + product) * sea[rows]).astype(BF16)
        act_grad = rdot(ups[cells, :], down[...])
        deriv = half + 0.5 * pre * (1.0 - tanh_val * tanh_val) * SLOPE * (1.0 + 3.0 * CUBIC * square)
        pre_grad = (act_grad * deriv).astype(BF16)
        pregrad[cells, :] = pre_grad
        nig = rdot(pre_grad, up[...])
        scaled = nig * gain_row
        nacc[0] += jnp.sum((nig * unit).reshape(32, 8, 128), 0)
        nacc[1] += jnp.sum(nig.reshape(32, 8, 128), 0)
        mg = rstd * (
            scaled
            - jnp.mean(scaled, -1, keepdims=True)
            - unit * jnp.mean(scaled * unit, -1, keepdims=True)
        )
        mp[0, rows, 1:9] = mg.reshape(4, 8, 8, 128)
        return carry

    zero_block = jnp.zeros((1, 8, 128), F32)

    def spread_row(r, carry):
        mp[0, r, 0:1] = zero_block
        blocks = jnp.concatenate([zero_block, mp[0, r, 1:9], zero_block], 0)
        for k, moved in enumerate(phases_of(blocks)):
            mp[k + 1, r] = moved
        return carry

    lax.fori_loop(0, 2, group, 0)
    halo_wait_recv(g, ext, fr, NORTH)

    flip = (
        lax.broadcasted_iota(jnp.int32, (80, 80), 0)
        + lax.broadcasted_iota(jnp.int32, (80, 80), 1)
        == 79
    ).astype(F32).astype(BF16)

    @pl.when(jnp.logical_not(g.north))
    def _():
        lax.fori_loop(16 + REACH, 16 + 2 * REACH, widen_row, 0)

    @pl.when(g.north)
    def _():
        def turn_row(k, carry):
            row = ext[16 + REACH + k].astype(F32).reshape(80, 128).astype(BF16)
            turned = jnp.dot(flip, row, preferred_element_type=F32).reshape(10, 8, 128)
            r = 16 + 2 * REACH - 1 - k
            ep[0, r] = turned
            for s, moved in enumerate(phases_of(turned)):
                ep[s + 1, r, 0:9] = moved
            return carry

        lax.fori_loop(0, REACH, turn_row, 0)

    lax.fori_loop(2, 4, group, 0)
    lax.fori_loop(0, 16, spread_row, 0)

    def eg_row(p, first, last):
        lo = jnp.zeros((9, 8, 128), F32)
        hi = jnp.zeros((9, 8, 128), F32)
        for i in range(first, last + 1):
            for j in range(KERNEL):
                off = 14 - 2 * j
                ph, skip = (off % 8) // 2, off // 8
                term = kt[i * KERNEL + j][None] * mp[ph, p - 2 * i]
                if skip:
                    lo = lo + term
                else:
                    hi = hi + term
        return jnp.concatenate([lo, zero_block], 0) + jnp.concatenate([zero_block, hi], 0)

    def eg_halo(start, first, last):
        def one(p, carry):
            egs[p] = eg_row(p, first, last).astype(BF16)
            return carry

        lax.fori_loop(start, start + 2, one, 0)

    def eg_center(start, stop, first, last):
        def one(p, carry):
            value = eg_row(p, first, last)
            eg[p - REACH] = value[1:9]
            egs[p, 0:1] = value[0:1].astype(BF16)
            egs[p, 9:10] = value[9:10].astype(BF16)
            return carry

        lax.fori_loop(start, stop, one, 0)

    for m in range(3):
        eg_halo(22 + 2 * m, 4 + m, 6)
    halo_start(g, egs, rb, BWD_ROWS, BWD_COLS, bs, br, (NORTH,))
    for m in range(3):
        eg_halo(2 * m, 0, m)
    halo_start(g, egs, rb, BWD_ROWS, BWD_COLS, bs, br, (SOUTH,))

    chunk = 512 // g.planes
    per = 128 // chunk
    up_part = tdot(normed[...], pregrad[...]).astype(BF16)
    pay1[0:per] = up_part[:, 0:128].reshape(per, chunk, 128)
    pay1[per : 2 * per] = up_part[:, 128:256].reshape(per, chunk, 128)
    down_part = tdot(active[...], ups[...]).astype(BF16)
    pay1[2 * per : 4 * per] = down_part.reshape(2 * per, chunk, 128)
    ra1[g.plane] = pay1[g.plane]
    plane_send(g, lambda peer: pay1.at[peer], ra1, ar_s.at[0], ar_r.at[0])

    for m in range(3, 6):
        eg_center(2 * m, 2 * m + 2, 0, m)
    eg_center(12, 16, 0, 6)
    for m in range(3):
        eg_center(16 + 2 * m, 18 + 2 * m, 1 + m, 6)
    halo_start(g, egs, rb, BWD_ROWS, BWD_COLS, bs, br, (CENTER,))

    def tap_row(r, carry):
        grad = mp[0, r, 1:9]
        for i in range(KERNEL):
            for j in range(KERNEL):
                off = 2 + 2 * j
                ph, skip = (off % 8) // 2, off // 8
                kacc[i * KERNEL + j] += jnp.sum(grad * ep[ph, r + 2 * i, skip : skip + 8], 0)
        return carry

    lax.fori_loop(0, 16, tap_row, 0)

    small = 64 // g.planes
    pay2[...] = jnp.zeros_like(pay2)
    for t in range(TAPS + 2):
        value = kacc[t] if t < TAPS else nacc[t - TAPS]
        pay2[t // small, t % small : t % small + 1] = jnp.sum(value, 0, keepdims=True)
    ra2[g.plane] = pay2[g.plane]
    plane_send(g, lambda peer: pay2.at[peer], ra2, ar_s.at[1], ar_r.at[1])

    bulk_wait(ra1, g.planes - 1, ar_r.at[0])
    zb1[g.lon] = jnp.sum(ra1[...].astype(F32), 0).astype(BF16)
    lon_send(g, zb1, ar_s.at[2], ar_r.at[2])
    bulk_wait(ra2, g.planes - 1, ar_r.at[1])
    zb2[g.lon] = jnp.sum(ra2[...], 0)
    lon_send(g, zb2, ar_s.at[3], ar_r.at[3])

    halo_wait_recv(g, rb, br, CENTER)

    def edge_row(r, carry):
        eg[r, 0:1] += rb[r + REACH, 0:1].astype(F32)
        eg[r, 7:8] += rb[r + REACH, 9:10].astype(F32)
        return carry

    lax.fori_loop(0, 16, edge_row, 0)
    halo_wait_recv(g, rb, br, SOUTH)

    def fold_in(r, row):
        eg[r] += row[1:9]
        eg[r, 0:1] += row[0:1]
        eg[r, 7:8] += row[9:10]

    @pl.when(g.lat > 0)
    def _():
        def one(k, carry):
            fold_in(k, rb[k].astype(F32))
            return carry

        lax.fori_loop(0, REACH, one, 0)

    halo_wait_recv(g, rb, br, NORTH)

    @pl.when(jnp.logical_not(g.north))
    def _():
        def one(k, carry):
            fold_in(10 + k, rb[22 + k].astype(F32))
            return carry

        lax.fori_loop(0, REACH, one, 0)

    @pl.when(g.north)
    def _():
        def one(k, carry):
            row = rb[22 + k].astype(F32).reshape(80, 128).astype(BF16)
            fold_in(15 - k, jnp.dot(flip, row, preferred_element_type=F32).reshape(10, 8, 128))
            return carry

        lax.fori_loop(0, REACH, one, 0)

    def last_row(r, carry):
        field_grad[r] = ((cotangent[r].astype(F32) + eg[r]) * sea[r]).astype(BF16)
        return carry

    lax.fori_loop(0, 16, last_row, 0)

    bulk_wait(zb1, g.nlon - 1, ar_r.at[2])
    gb1[g.plane] = jnp.sum(zb1[...].astype(F32), 0).astype(BF16)
    plane_send(g, lambda peer: gb1.at[g.plane], gb1, ar_s.at[4], ar_r.at[4])
    bulk_wait(zb2, g.nlon - 1, ar_r.at[3])
    gb2[g.plane] = jnp.sum(zb2[...], 0)
    plane_send(g, lambda peer: gb2.at[g.plane], gb2, ar_s.at[5], ar_r.at[5])

    bulk_wait(gb1, g.planes - 1, ar_r.at[4])
    up_grad[:, 0:128] = gb1[0:per].astype(F32).reshape(128, 128) * factor
    up_grad[:, 128:256] = gb1[per : 2 * per].astype(F32).reshape(128, 128) * factor
    down_grad[...] = gb1[2 * per : 4 * per].astype(F32).reshape(256, 128) * factor
    bulk_wait(gb2, g.planes - 1, ar_r.at[5])
    for t in range(TAPS + 2):
        value = gb2[t // small, t % small : t % small + 1] * factor
        if t < TAPS:
            kernel_grad[t : t + 1, :] = value
        else:
            norm_grad[t - TAPS : t - TAPS + 1, :] = value

    halo_wait_send(g, ext, FWD_ROWS, FWD_COLS, fs)
    halo_wait_send(g, egs, BWD_ROWS, BWD_COLS, bs)
    bulk_wait(pay1, g.planes - 1, ar_s.at[0])
    bulk_wait(pay2, g.planes - 1, ar_s.at[1])
    bulk_wait(zb1, g.nlon - 1, ar_s.at[2])
    bulk_wait(zb2, g.nlon - 1, ar_s.at[3])
    bulk_wait(gb1, g.planes - 1, ar_s.at[4])
    bulk_wait(gb2, g.planes - 1, ar_s.at[5])


def shards(sizes, field, cotangent, land_mask, kernel_taps, norm_gain, norm_shift, up_weight, down_weight):
    planes = sizes[1] * sizes[2]
    chunk, small = 512 // planes, 64 // planes
    tile = (16, 8, 8, 128)
    vmem = pl.BlockSpec(memory_space=pltpu.VMEM)
    dma = pltpu.SemaphoreType.DMA
    out = pl.pallas_call(
        functools.partial(kernel, sizes),
        out_shape=(
            jax.ShapeDtypeStruct(tile, BF16),
            jax.ShapeDtypeStruct(tile, BF16),
            jax.ShapeDtypeStruct((TAPS, 128), F32),
            jax.ShapeDtypeStruct((2, 128), F32),
            jax.ShapeDtypeStruct((128, 256), F32),
            jax.ShapeDtypeStruct((256, 128), F32),
        ),
        in_specs=[vmem] * 8,
        out_specs=(vmem,) * 6,
        scratch_shapes=[
            pltpu.VMEM((28, 10, 8, 128), BF16),
            pltpu.VMEM(tile, F32),
            pltpu.VMEM((4, 28, 10, 8, 128), F32),
            pltpu.VMEM((TAPS, 8, 128), F32),
            pltpu.VMEM((1024, 128), BF16),
            pltpu.VMEM((1024, 128), F32),
            pltpu.VMEM((1024, 128), BF16),
            pltpu.VMEM((1024, 256), BF16),
            pltpu.VMEM((1024, 256), BF16),
            pltpu.VMEM((2, 8, 128), F32),
            pltpu.VMEM((4, 16, 9, 8, 128), F32),
            pltpu.VMEM((TAPS, 8, 128), F32),
            pltpu.VMEM(tile, F32),
            pltpu.VMEM((28, 10, 8, 128), BF16),
            pltpu.VMEM((28, 10, 8, 128), BF16),
            pltpu.VMEM((planes, chunk, 128), BF16),
            pltpu.VMEM((planes, chunk, 128), BF16),
            pltpu.VMEM((sizes[0], chunk, 128), BF16),
            pltpu.VMEM((planes, chunk, 128), BF16),
            pltpu.VMEM((planes, small, 128), F32),
            pltpu.VMEM((planes, small, 128), F32),
            pltpu.VMEM((sizes[0], small, 128), F32),
            pltpu.VMEM((planes, small, 128), F32),
            dma((9,)),
            dma((9,)),
            dma((9,)),
            dma((9,)),
            dma((6,)),
            dma((6,)),
        ],
        compiler_params=pltpu.CompilerParams(
            collective_id=0, has_side_effects=True, vmem_limit_bytes=48 * 1024 * 1024
        ),
        name="ocean_block",
    )(
        field.reshape(tile),
        cotangent.reshape(tile),
        land_mask,
        kernel_taps,
        norm_gain.reshape(1, 128),
        norm_shift.reshape(1, 128),
        up_weight,
        down_weight,
    )
    return (out[0].reshape(field.shape), out[1].reshape(field.shape)) + tuple(out[2:])


def solution(mesh):
    sizes = (mesh.shape["lon"], mesh.shape["lat"], mesh.shape["ens"])
    tiles = P("ens", "lat", "lon", None)
    in_specs = (tiles, tiles, P("lat", "lon"), P(), P(), P(), P(), P())
    out_specs = (tiles, tiles, P(), P(), P(), P())
    return jax.shard_map(
        functools.partial(shards, sizes),
        mesh=mesh,
        in_specs=in_specs,
        out_specs=out_specs,
        check_vma=False,
    )
```

time: 699 us -> 69.8 us (0.10)
  waiting for transfers between devices: 467 us -> 0 us
  blocking collectives: 106 us -> 0 us
  starting transfers between devices: 78.3 us -> 0 us
  Pallas kernels: 0 us -> 59.2 us
  other arithmetic: 27.3 us -> 0 us
  between operations: 14.5 us -> 0.67 us
  local copies, waits for them, and re-layouts: 1.09 us -> 9.56 us
    psum x1 -> x0, waiting for transfers between devices: 445 us -> none  [shards(): lax.psum((kernel_part, norm_part, up_part, down_part), ('lon', 'lat', 'en...]
    psum x1 -> x0, blocking collectives: 106 us -> none  [shards(): lax.psum((kernel_part, norm_part, up_part, down_part), ('lon', 'lat', 'en...]
    ppermute x16 -> x0, starting transfers between devices: 78.3 us -> none  [the longest x8 54.1 us: partner(): lax.ppermute(shard, axis, [(i, i ^ 1 << bit) for i in range(lax.axis_size...]
    pallas_call x0 -> x1, Pallas kernels: none -> 59.2 us  [shards(): pl.pallas_call(functools.partial(kernel, sizes), out_shape=(jax.ShapeDtyp...]
    ppermute x16 -> x0, waiting for transfers between devices: 21.9 us -> none  [the longest x8 20.7 us: partner(): lax.ppermute(shard, axis, [(i, i ^ 1 << bit) for i in range(lax.axis_size...]
    another operation x2 -> x0, other arithmetic: 10.4 us -> none
    unnamed x16 -> x22, local copies, waits for them, and re-layouts: 0.05 us -> 9.56 us
    reduce_sum x6 -> x0, other arithmetic: 7.89 us -> none  [the longest x1 3.95 us: shards(): centered = mixed - jnp.mean(mixed, -1, keepdims=True)]
  transfers between devices with their start and end apart: 17 -> 0, of which waited for: 7 -> 0; matrix products, arithmetic and copies ran while one was open for 1% -> 0% of each run, Pallas kernels for 0% -> 0%
where the time goes in v1:
time: 69.8 us; the launch traced here: 69.4 us
  Pallas kernels  59.2 us (85%)
  local copies, waits for them, and re-layouts  9.56 us (14%)
    pallas_call x1, Pallas kernels, shards(): pl.pallas_call(functools.partial(kernel, sizes), out_shape=(jax.ShapeDtyp...  59.2 us
    unnamed x22, local copies, waits for them, and re-layouts  9.56 us

profile of v1, /device:TPU:1, one launch (start us, length us, event | category | flops | bytes accessed | tf_op | source)
XLA Modules:
  0.0 69.4 jit_solution(3509861264119528898)
XLA Ops:
  0.6 0.0 copy-start.6
  0.6 0.0 copy-start.7
  0.7 0.6 copy-done.6
  1.3 0.0 copy-done.7
  1.3 0.0 copy-start
  1.3 0.9 %copy-done = bf16[1,16,64,128]{3,2,1,0:T(8,128)(2,1)S(1)} copy-done((bf16[1,16,64,128]{3,2,1,0:T(8,128)(2,1)S(1)}, bf16[1,16,64,128]{3,2,1,0:T(8,128)(2,1)}, u32[]{:S(2)}) %copy-start) | copy-done | bytes 262168
  2.3 0.0 copy-start.1
  2.3 0.9 %copy-done.1 = bf16[1,16,64,128]{3,2,1,0:T(8,128)(2,1)S(1)} copy-done((bf16[1,16,64,128]{3,2,1,0:T(8,128)(2,1)S(1)}, bf16[1,16,64,128]{3,2,1,0:T(8,128)(2,1)}, u32[]{:S(2)}) %copy-start.1) | copy-done | bytes 262168
  3.2 0.0 copy-start.2
  3.2 0.8 %copy-done.2 = bf16[128,256]{1,0:T(8,128)(2,1)S(1)} copy-done((bf16[128,256]{1,0:T(8,128)(2,1)S(1)}, bf16[128,256]{1,0:T(8,128)(2,1)}, u32[]{:S(2)}) %copy-start.2) | copy-done | bytes 65560
  4.0 0.0 copy-start.3
  4.0 0.8 %copy-done.3 = bf16[256,128]{1,0:T(8,128)(2,1)S(1)} copy-done((bf16[256,128]{1,0:T(8,128)(2,1)S(1)}, bf16[256,128]{1,0:T(8,128)(2,1)}, u32[]{:S(2)}) %copy-start.3) | copy-done | bytes 65560
  4.9 0.0 copy-start.4
  4.9 0.7 %copy-done.4 = f32[49,128]{1,0:T(8,128)S(1)} copy-done((f32[49,128]{1,0:T(8,128)S(1)}, f32[49,128]{1,0:T(8,128)}, u32[]{:S(2)}) %copy-start.4) | copy-done | bytes 25112
  5.6 0.0 copy-start.5
  5.6 0.7 %copy-done.5 = s32[16,64]{1,0:T(8,128)S(1)} copy-done((s32[16,64]{1,0:T(8,128)S(1)}, s32[16,64]{1,0:T(8,128)}, u32[]{:S(2)}) %copy-start.5) | copy-done | bytes 4120
  6.3 59.2 %ocean_block.1 = (bf16[16,8,8,128]{3,2,1,0:T(8,128)(2,1)S(1)}, bf16[16,8,8,128]{3,2,1,0:T(8,128)(2,1)S(1)}, f32[49,128]{1,0:T(8,128)S(1)}, f32[2,128]{1,0:T(2,12...) custom-call(bf16[16,8,8,128]{3,2,1,0:T(8,128)(2,1)S(1)} %bitcast.6, bf16[16,8,8,128]{3,2,1,0:T(8,128)(2,1)S(1)} %bitcast.7, ...), custom_call_target="tpu_custom_call" | custom-call | tf_op jit(solution)/shard_map/ocean_block/pallas_call | solution.py:519
  65.5 0.7 %copy.20 = bf16[1,16,64,128]{3,2,1,0:T(8,128)(2,1)} copy(bf16[1,16,64,128]{3,2,1,0:T(8,128)(2,1)S(1)} %bitcast.9) | data formatting | bytes 524288
  66.3 0.7 %copy.21 = bf16[1,16,64,128]{3,2,1,0:T(8,128)(2,1)} copy(bf16[1,16,64,128]{3,2,1,0:T(8,128)(2,1)S(1)} %bitcast.8) | data formatting | bytes 524288
  67.0 0.6 copy.22
  67.6 0.6 copy.23
  68.1 0.7 copy.24
  68.8 0.7 copy.25
Async XLA Ops:
  0.6 0.7 copy-start.6
  0.6 0.7 copy-start.7
  1.3 0.9 %copy-start = (bf16[1,16,64,128]{3,2,1,0:T(8,128)(2,1)S(1)}, bf16[1,16,64,128]{3,2,1,0:T(8,128)(2,1)}, u32[]{:S(2)}) copy-start(bf16[1,16,64,128]{3,2,1,0:T(8,128)(2,1)} %param.8) | copy-start | bytes 786436
  2.3 0.9 %copy-start.1 = (bf16[1,16,64,128]{3,2,1,0:T(8,128)(2,1)S(1)}, bf16[1,16,64,128]{3,2,1,0:T(8,128)(2,1)}, u32[]{:S(2)}) copy-start(bf16[1,16,64,128]{3,2,1,0:T(8,128)(2,1)} %param.9) | copy-start | bytes 786436
  3.2 0.8 %copy-start.2 = (bf16[128,256]{1,0:T(8,128)(2,1)S(1)}, bf16[128,256]{1,0:T(8,128)(2,1)}, u32[]{:S(2)}) copy-start(bf16[128,256]{1,0:T(8,128)(2,1)} %up.1) | copy-start | bytes 196612
  4.0 0.8 %copy-start.3 = (bf16[256,128]{1,0:T(8,128)(2,1)S(1)}, bf16[256,128]{1,0:T(8,128)(2,1)}, u32[]{:S(2)}) copy-start(bf16[256,128]{1,0:T(8,128)(2,1)} %down.1) | copy-start | bytes 196612
  4.9 0.7 %copy-start.4 = (f32[49,128]{1,0:T(8,128)S(1)}, f32[49,128]{1,0:T(8,128)}, u32[]{:S(2)}) copy-start(f32[49,128]{1,0:T(8,128)} %taps.1) | copy-start | bytes 75268
  5.6 0.7 %copy-start.5 = (s32[16,64]{1,0:T(8,128)S(1)}, s32[16,64]{1,0:T(8,128)}, u32[]{:S(2)}) copy-start(s32[16,64]{1,0:T(8,128)} %mask.1) | copy-start | bytes 12292

commit v2 on v1

--- a/solution.py
+++ b/solution.py
@@ -57,10 +57,25 @@
         self.north = self.lat == nlat - 1
         self.plane = self.lat * nens + self.ens
         self.planes = nlat * nens
+        self.owners = min(8, self.planes)
+        across, along = nlat // 2, nens // 2 * 2
+        y = self.ens // 2 * 2 + lax.rem(self.lat, 2)
+        core = lax.rem(self.ens, 2)
+        xs = [lax.rem(self.lat // 2 + d, across) for d in range(across)]
+        ys = [lax.rem(y + d, along) for d in range(along)]
+        steps = [(dx, dy, dc) for dx in range(across) for dy in range(along) for dc in range(2)][1:]
+        steps.sort(key=lambda s: -min(s[0], across - s[0]) - min(s[1], along - s[1]))
+        self.peers = []
+        for dx, dy, dc in steps:
+            lat = xs[dx] * 2 + lax.rem(ys[dy], 2)
+            ens = ys[dy] // 2 * 2 + (1 - core if dc else core)
+            self.peers.append((lat, ens))
+        far = sorted(range(1, nlon), key=lambda k: -min(k, nlon - k))
+        self.lons = [lax.rem(self.lon + k, nlon) for k in far]
 
 
 def halo_start(g, src, dst, src_rows, src_cols, ssem, rsem, only_rows):
-    for rr, cc in REGIONS:
+    for rr, cc in sorted(REGIONS, key=lambda rc: only_rows.index(rc[0]) if rc[0] in only_rows else 9):
         if rr not in only_rows:
             continue
         here = region(src, src_rows[rr], src_cols[cc])
@@ -136,34 +151,42 @@
 
 
 def plane_send(g, src_of, dst, ssem, rsem):
-    def one(k, carry):
-        peer = lax.rem(g.plane + k, g.planes)
+    for lat, ens in g.peers:
         pltpu.make_async_remote_copy(
-            src_ref=src_of(peer),
+            src_ref=src_of(lat * g.nens + ens),
             dst_ref=dst.at[g.plane],
             send_sem=ssem,
             recv_sem=rsem,
-            device_id={"lat": peer // g.nens, "ens": lax.rem(peer, g.nens)},
+            device_id={"lat": lat, "ens": ens},
             device_id_type=MESH,
         ).start()
-        return carry
-
-    lax.fori_loop(1, g.planes, one, 0)
+
+
+def owner_send(g, src, dst, ssem, rsem):
+    for o in range(g.owners):
+
+        @pl.when(g.plane != o)
+        def _(o=o):
+            pltpu.make_async_remote_copy(
+                src_ref=src.at[o],
+                dst_ref=dst.at[g.plane],
+                send_sem=ssem,
+                recv_sem=rsem,
+                device_id={"lat": o // g.nens, "ens": o % g.nens},
+                device_id_type=MESH,
+            ).start()
 
 
 def lon_send(g, buf, ssem, rsem):
-    def one(k, carry):
+    for lon in g.lons:
         pltpu.make_async_remote_copy(
             src_ref=buf.at[g.lon],
             dst_ref=buf.at[g.lon],
             send_sem=ssem,
             recv_sem=rsem,
-            device_id={"lon": lax.rem(g.lon + k, g.nlon)},
+            device_id={"lon": lon},
             device_id_type=MESH,
         ).start()
-        return carry
-
-    lax.fori_loop(1, g.nlon, one, 0)
 
 
 def bulk_wait(buf, count, sem):
@@ -179,28 +202,40 @@
 
 def kernel(
     sizes,
+    field_h, cotangent_h, mask_h, taps_h, gain_h, shift_h, up_h, down_h,
+    output, field_grad, kernel_grad, norm_grad, up_grad, down_grad,
     field, cotangent, mask, taps, gain, shift, up, down,
-    output, field_grad, kernel_grad, norm_grad, up_grad, down_grad,
-    ext, sea, ep, kt, ups, mixed, normed, active, pregrad, nacc, mp, kacc, eg, egs, rb,
+    ext, sea, ep, kt, ups, mixed, normed, active, pregrad, mp, kacc, uacc, dacc, eg, egs, rb,
     pay1, ra1, zb1, gb1, pay2, ra2, zb2, gb2,
-    fs, fr, bs, br, ar_s, ar_r,
+    ins, fs, fr, bs, br, ar_s, ar_r,
 ):
     g = Grid(*sizes)
     factor = 1.0 / math.sqrt(1024 * g.nlon * g.nlat * g.nens)
+    owner = g.plane < g.owners
+
+    loads = {}
+    for k, (name, src, dst) in enumerate(
+        (
+            ("mask", mask_h, mask),
+            ("field", field_h, field),
+            ("cotangent", cotangent_h, cotangent),
+            ("taps", taps_h, taps),
+            ("gain", gain_h, gain),
+            ("shift", shift_h, shift),
+            ("up", up_h, up),
+            ("down", down_h, down),
+        )
+    ):
+        loads[name] = pltpu.make_async_copy(src, dst, ins.at[k])
+        loads[name].start()
 
     barrier = pltpu.get_barrier_semaphore()
 
     def greet(**where):
         pl.semaphore_signal(barrier, inc=1, device_id=where, device_id_type=MESH)
 
-    def greet_plane(k, carry):
-        peer = lax.rem(g.plane + k, g.planes)
-        greet(lat=peer // g.nens, ens=lax.rem(peer, g.nens))
-        return carry
-
-    def greet_lon(k, carry):
-        greet(lon=lax.rem(g.lon + k, g.nlon))
-        return carry
+    for lon in g.lons:
+        greet(lon=lon)
 
     east = lax.rem(g.lon + 1, g.nlon)
     west = lax.rem(g.lon + g.nlon - 1, g.nlon)
@@ -215,38 +250,39 @@
         greet(lat=g.lat + 1, lon=east)
         greet(lat=g.lat + 1, lon=west)
 
-    lax.fori_loop(1, g.planes, greet_plane, 0)
-    lax.fori_loop(1, g.nlon, greet_lon, 0)
+    for lat, ens in g.peers:
+        greet(lat=lat, ens=ens)
 
     eye = (
         lax.broadcasted_iota(jnp.int32, (64, 64), 0) == lax.broadcasted_iota(jnp.int32, (64, 64), 1)
     )
     ones = jnp.ones((64, 128), BF16)
-
-    def mask_row(r, carry):
-        marks = jnp.broadcast_to(mask[pl.ds(r, 1), :].astype(F32), (64, 64))
+    loads["mask"].wait()
+    loads["field"].wait()
+    for r in range(16):
+        marks = jnp.broadcast_to(mask[r : r + 1, :].astype(F32), (64, 64))
         spread = jnp.where(eye, marks, 0.0).astype(BF16)
         wide = jnp.dot(spread, ones, preferred_element_type=F32).reshape(8, 8, 128)
         sea[r] = wide
         ext[r + REACH, 1:9] = (field[r].astype(F32) * wide).astype(BF16)
-        return carry
-
-    lax.fori_loop(0, 16, mask_row, 0)
 
     count = g.planes + g.nlon - 2
     count = count + 2 * (g.lat > 0).astype(jnp.int32) + 2 * (g.lat < g.nlat - 1).astype(jnp.int32)
     pl.semaphore_wait(barrier, count)
-    halo_start(g, ext, ext, FWD_ROWS, FWD_COLS, fs, fr, (NORTH, SOUTH, CENTER))
+    halo_start(g, ext, ext, FWD_ROWS, FWD_COLS, fs, fr, (CENTER, NORTH, SOUTH))
+
+    loads["cotangent"].wait()
+    for name in ("taps", "gain", "shift", "up", "down"):
+        loads[name].wait()
 
     def upstream_row(r, carry):
         wide = cotangent[r].astype(F32) * sea[r]
         ups[pl.ds(pl.multiple_of(r * 64, 64), 64), :] = wide.reshape(64, 128).astype(BF16)
         return carry
 
-    lax.fori_loop(0, 16, upstream_row, 0)
+    lax.fori_loop(0, 16, upstream_row, 0, unroll=4)
     for t in range(TAPS):
         kt[t] = jnp.broadcast_to(taps[t : t + 1, :], (8, 128))
-    nacc[...] = jnp.zeros_like(nacc)
     kacc[...] = jnp.zeros_like(kacc)
 
     def widen_row(r, carry):
@@ -280,9 +316,10 @@
     gain_row = gain[...]
     shift_row = shift[...]
 
-    def group(q, carry):
-        lax.fori_loop(4 * q, 4 * q + 4, conv_row, 0)
-        cells = pl.ds(pl.multiple_of(q * 256, 256), 256)
+    def group(first, many):
+        lax.fori_loop(first, first + many, conv_row, 0)
+        cells = slice(64 * first, 64 * (first + many))
+        rows = slice(first, first + many)
         x = mixed[cells, :]
         centered = x - jnp.mean(x, -1, keepdims=True)
         rstd = lax.rsqrt(jnp.mean(centered * centered, -1, keepdims=True) + 1e-06)
@@ -291,28 +328,27 @@
         normed[cells, :] = norm
         pre = jnp.dot(norm, up[...], preferred_element_type=F32)
         square = pre * pre
-        tanh_val = jnp.tanh(SLOPE * (pre + CUBIC * pre * square))
-        half = 0.5 * (1.0 + tanh_val)
-        act = (pre * half).astype(BF16)
+        tanh_val = jnp.tanh(pre * (SLOPE + (SLOPE * CUBIC) * square))
+        half = 0.5 + 0.5 * tanh_val
+        gated = pre * half
+        act = gated.astype(BF16)
         active[cells, :] = act
-        product = jnp.dot(act, down[...], preferred_element_type=F32).reshape(4, 8, 8, 128)
-        rows = pl.ds(4 * q, 4)
+        product = jnp.dot(act, down[...], preferred_element_type=F32).reshape(many, 8, 8, 128)
         output[rows] = ((field[rows].astype(F32) + product) * sea[rows]).astype(BF16)
         act_grad = rdot(ups[cells, :], down[...])
-        deriv = half + 0.5 * pre * (1.0 - tanh_val * tanh_val) * SLOPE * (1.0 + 3.0 * CUBIC * square)
+        deriv = half + gated * (1.0 - tanh_val) * (SLOPE + (3.0 * SLOPE * CUBIC) * square)
         pre_grad = (act_grad * deriv).astype(BF16)
         pregrad[cells, :] = pre_grad
         nig = rdot(pre_grad, up[...])
         scaled = nig * gain_row
-        nacc[0] += jnp.sum((nig * unit).reshape(32, 8, 128), 0)
-        nacc[1] += jnp.sum(nig.reshape(32, 8, 128), 0)
+        kacc[TAPS] += jnp.sum((nig * unit).reshape(8 * many, 8, 128), 0)
+        kacc[TAPS + 1] += jnp.sum(nig.reshape(8 * many, 8, 128), 0)
         mg = rstd * (
             scaled
             - jnp.mean(scaled, -1, keepdims=True)
             - unit * jnp.mean(scaled * unit, -1, keepdims=True)
         )
-        mp[0, rows, 1:9] = mg.reshape(4, 8, 8, 128)
-        return carry
+        mp[0, rows, 1:9] = mg.reshape(many, 8, 8, 128)
 
     zero_block = jnp.zeros((1, 8, 128), F32)
 
@@ -323,7 +359,21 @@
             mp[k + 1, r] = moved
         return carry
 
-    lax.fori_loop(0, 2, group, 0)
+    def tap_row(r, carry):
+        grad = mp[0, r, 1:9]
+        for i in range(KERNEL):
+            for j in range(KERNEL):
+                off = 2 + 2 * j
+                ph, skip = (off % 8) // 2, off // 8
+                kacc[i * KERNEL + j] += jnp.sum(grad * ep[ph, r + 2 * i, skip : skip + 8], 0)
+        return carry
+
+    group(0, 5)
+    group(5, 5)
+    lax.fori_loop(0, 10, tap_row, 0)
+    lax.fori_loop(0, 10, spread_row, 0)
+    uacc[...] = tdot(normed[0:640, :], pregrad[0:640, :])
+    dacc[...] = tdot(active[0:640, :], ups[0:640, :])
     halo_wait_recv(g, ext, fr, NORTH)
 
     flip = (
@@ -338,19 +388,16 @@
 
     @pl.when(g.north)
     def _():
-        def turn_row(k, carry):
+        for k in range(REACH):
             row = ext[16 + REACH + k].astype(F32).reshape(80, 128).astype(BF16)
             turned = jnp.dot(flip, row, preferred_element_type=F32).reshape(10, 8, 128)
             r = 16 + 2 * REACH - 1 - k
             ep[0, r] = turned
             for s, moved in enumerate(phases_of(turned)):
                 ep[s + 1, r, 0:9] = moved
-            return carry
-
-        lax.fori_loop(0, REACH, turn_row, 0)
-
-    lax.fori_loop(2, 4, group, 0)
-    lax.fori_loop(0, 16, spread_row, 0)
+
+    group(10, 6)
+    lax.fori_loop(10, 16, spread_row, 0)
 
     def eg_row(p, first, last):
         lo = jnp.zeros((9, 8, 128), F32)
@@ -386,20 +433,30 @@
     for m in range(3):
         eg_halo(22 + 2 * m, 4 + m, 6)
     halo_start(g, egs, rb, BWD_ROWS, BWD_COLS, bs, br, (NORTH,))
+
+    chunk = 512 // g.planes
+    per = 128 // chunk
+    up_part = (uacc[...] + tdot(normed[640:1024, :], pregrad[640:1024, :])).astype(BF16)
+    pay1[0:per] = up_part[:, 0:128].reshape(per, chunk, 128)
+    pay1[per : 2 * per] = up_part[:, 128:256].reshape(per, chunk, 128)
+    down_part = (dacc[...] + tdot(active[640:1024, :], ups[640:1024, :])).astype(BF16)
+    pay1[2 * per : 4 * per] = down_part.reshape(2 * per, chunk, 128)
+    ra1[g.plane] = pay1[g.plane]
+    plane_send(g, lambda peer: pay1.at[peer], ra1, ar_s.at[0], ar_r.at[0])
+
+    lax.fori_loop(10, 16, tap_row, 0)
+    small = 64 // g.owners
+    pay2[...] = jnp.sum(kacc[...], 1).reshape(g.owners, small, 128)
+
+    @pl.when(owner)
+    def _():
+        ra2[g.plane] = pay2[g.plane]
+
+    owner_send(g, pay2, ra2, ar_s.at[1], ar_r.at[1])
+
     for m in range(3):
         eg_halo(2 * m, 0, m)
     halo_start(g, egs, rb, BWD_ROWS, BWD_COLS, bs, br, (SOUTH,))
-
-    chunk = 512 // g.planes
-    per = 128 // chunk
-    up_part = tdot(normed[...], pregrad[...]).astype(BF16)
-    pay1[0:per] = up_part[:, 0:128].reshape(per, chunk, 128)
-    pay1[per : 2 * per] = up_part[:, 128:256].reshape(per, chunk, 128)
-    down_part = tdot(active[...], ups[...]).astype(BF16)
-    pay1[2 * per : 4 * per] = down_part.reshape(2 * per, chunk, 128)
-    ra1[g.plane] = pay1[g.plane]
-    plane_send(g, lambda peer: pay1.at[peer], ra1, ar_s.at[0], ar_r.at[0])
-
     for m in range(3, 6):
         eg_center(2 * m, 2 * m + 2, 0, m)
     eg_center(12, 16, 0, 6)
@@ -407,31 +464,15 @@
         eg_center(16 + 2 * m, 18 + 2 * m, 1 + m, 6)
     halo_start(g, egs, rb, BWD_ROWS, BWD_COLS, bs, br, (CENTER,))
 
-    def tap_row(r, carry):
-        grad = mp[0, r, 1:9]
-        for i in range(KERNEL):
-            for j in range(KERNEL):
-                off = 2 + 2 * j
-                ph, skip = (off % 8) // 2, off // 8
-                kacc[i * KERNEL + j] += jnp.sum(grad * ep[ph, r + 2 * i, skip : skip + 8], 0)
-        return carry
-
-    lax.fori_loop(0, 16, tap_row, 0)
-
-    small = 64 // g.planes
-    pay2[...] = jnp.zeros_like(pay2)
-    for t in range(TAPS + 2):
-        value = kacc[t] if t < TAPS else nacc[t - TAPS]
-        pay2[t // small, t % small : t % small + 1] = jnp.sum(value, 0, keepdims=True)
-    ra2[g.plane] = pay2[g.plane]
-    plane_send(g, lambda peer: pay2.at[peer], ra2, ar_s.at[1], ar_r.at[1])
-
     bulk_wait(ra1, g.planes - 1, ar_r.at[0])
     zb1[g.lon] = jnp.sum(ra1[...].astype(F32), 0).astype(BF16)
     lon_send(g, zb1, ar_s.at[2], ar_r.at[2])
-    bulk_wait(ra2, g.planes - 1, ar_r.at[1])
-    zb2[g.lon] = jnp.sum(ra2[...], 0)
-    lon_send(g, zb2, ar_s.at[3], ar_r.at[3])
+
+    @pl.when(owner)
+    def _():
+        bulk_wait(ra2, g.planes - 1, ar_r.at[1])
+        zb2[g.lon] = jnp.sum(ra2[...], 0)
+        lon_send(g, zb2, ar_s.at[3], ar_r.at[3])
 
     halo_wait_recv(g, rb, br, CENTER)
 
@@ -468,67 +509,103 @@
 
     @pl.when(g.north)
     def _():
-        def one(k, carry):
+        for k in range(REACH):
             row = rb[22 + k].astype(F32).reshape(80, 128).astype(BF16)
             fold_in(15 - k, jnp.dot(flip, row, preferred_element_type=F32).reshape(10, 8, 128))
-            return carry
-
-        lax.fori_loop(0, REACH, one, 0)
 
     def last_row(r, carry):
         field_grad[r] = ((cotangent[r].astype(F32) + eg[r]) * sea[r]).astype(BF16)
         return carry
 
-    lax.fori_loop(0, 16, last_row, 0)
+    lax.fori_loop(0, 16, last_row, 0, unroll=2)
 
     bulk_wait(zb1, g.nlon - 1, ar_r.at[2])
     gb1[g.plane] = jnp.sum(zb1[...].astype(F32), 0).astype(BF16)
     plane_send(g, lambda peer: gb1.at[g.plane], gb1, ar_s.at[4], ar_r.at[4])
-    bulk_wait(zb2, g.nlon - 1, ar_r.at[3])
-    gb2[g.plane] = jnp.sum(zb2[...], 0)
-    plane_send(g, lambda peer: gb2.at[g.plane], gb2, ar_s.at[5], ar_r.at[5])
+
+    @pl.when(owner)
+    def _():
+        bulk_wait(zb2, g.nlon - 1, ar_r.at[3])
+        gb2[g.plane] = jnp.sum(zb2[...], 0)
+        plane_send(g, lambda peer: gb2.at[g.plane], gb2, ar_s.at[5], ar_r.at[5])
 
     bulk_wait(gb1, g.planes - 1, ar_r.at[4])
     up_grad[:, 0:128] = gb1[0:per].astype(F32).reshape(128, 128) * factor
     up_grad[:, 128:256] = gb1[per : 2 * per].astype(F32).reshape(128, 128) * factor
     down_grad[...] = gb1[2 * per : 4 * per].astype(F32).reshape(256, 128) * factor
-    bulk_wait(gb2, g.planes - 1, ar_r.at[5])
-    for t in range(TAPS + 2):
-        value = gb2[t // small, t % small : t % small + 1] * factor
-        if t < TAPS:
-            kernel_grad[t : t + 1, :] = value
-        else:
-            norm_grad[t - TAPS : t - TAPS + 1, :] = value
+
+    @pl.when(owner)
+    def _():
+        bulk_wait(gb2, g.owners - 1, ar_r.at[5])
+
+    @pl.when(jnp.logical_not(owner))
+    def _():
+        bulk_wait(gb2, g.owners, ar_r.at[5])
+
+    small_sums = gb2[...].reshape(64, 128) * factor
+    kernel_grad[...] = small_sums[0:TAPS]
+    norm_grad[...] = small_sums[TAPS : TAPS + 2]
 
     halo_wait_send(g, ext, FWD_ROWS, FWD_COLS, fs)
     halo_wait_send(g, egs, BWD_ROWS, BWD_COLS, bs)
     bulk_wait(pay1, g.planes - 1, ar_s.at[0])
-    bulk_wait(pay2, g.planes - 1, ar_s.at[1])
     bulk_wait(zb1, g.nlon - 1, ar_s.at[2])
-    bulk_wait(zb2, g.nlon - 1, ar_s.at[3])
     bulk_wait(gb1, g.planes - 1, ar_s.at[4])
-    bulk_wait(gb2, g.planes - 1, ar_s.at[5])
+
+    @pl.when(owner)
+    def _():
+        bulk_wait(pay2, g.owners - 1, ar_s.at[1])
+        bulk_wait(zb2, g.nlon - 1, ar_s.at[3])
+        bulk_wait(ra2, g.planes - 1, ar_s.at[5])
+
+    @pl.when(jnp.logical_not(owner))
+    def _():
+        bulk_wait(pay2, g.owners, ar_s.at[1])
+
+
+def write_out(*refs):
+    sems = refs[-1]
+    half = len(refs) // 2
+    copies = [
+        pltpu.make_async_copy(src, dst, sems.at[k])
+        for k, (src, dst) in enumerate(zip(refs[:half], refs[half:-1]))
+    ]
+    for copy in copies:
+        copy.start()
+    for copy in copies:
+        copy.wait()
 
 
 def shards(sizes, field, cotangent, land_mask, kernel_taps, norm_gain, norm_shift, up_weight, down_weight):
     planes = sizes[1] * sizes[2]
-    chunk, small = 512 // planes, 64 // planes
+    owners = min(8, planes)
+    chunk, small = 512 // planes, 64 // owners
     tile = (16, 8, 8, 128)
     vmem = pl.BlockSpec(memory_space=pltpu.VMEM)
+    hbm = pl.BlockSpec(memory_space=pltpu.HBM)
     dma = pltpu.SemaphoreType.DMA
-    out = pl.pallas_call(
+    results = (
+        jax.ShapeDtypeStruct(tile, BF16),
+        jax.ShapeDtypeStruct(tile, BF16),
+        jax.ShapeDtypeStruct((TAPS, 128), F32),
+        jax.ShapeDtypeStruct((2, 128), F32),
+        jax.ShapeDtypeStruct((128, 256), F32),
+        jax.ShapeDtypeStruct((256, 128), F32),
+    )
+    held = pl.pallas_call(
         functools.partial(kernel, sizes),
-        out_shape=(
-            jax.ShapeDtypeStruct(tile, BF16),
-            jax.ShapeDtypeStruct(tile, BF16),
-            jax.ShapeDtypeStruct((TAPS, 128), F32),
-            jax.ShapeDtypeStruct((2, 128), F32),
-            jax.ShapeDtypeStruct((128, 256), F32),
-            jax.ShapeDtypeStruct((256, 128), F32),
-        ),
-        in_specs=[vmem] * 8,
+        out_shape=results,
+        in_specs=[hbm] * 8,
         out_specs=(vmem,) * 6,
         scratch_shapes=[
+            pltpu.VMEM(tile, BF16),
+            pltpu.VMEM(tile, BF16),
+            pltpu.VMEM((16, 64), jnp.int32),
+            pltpu.VMEM((TAPS, 128), F32),
+            pltpu.VMEM((1, 128), F32),
+            pltpu.VMEM((1, 128), F32),
+            pltpu.VMEM((128, 256), BF16),
+            pltpu.VMEM((256, 128), BF16),
             pltpu.VMEM((28, 10, 8, 128), BF16),
             pltpu.VMEM(tile, F32),
             pltpu.VMEM((4, 28, 10, 8, 128), F32),
@@ -538,9 +615,10 @@
             pltpu.VMEM((1024, 128), BF16),
             pltpu.VMEM((1024, 256), BF16),
             pltpu.VMEM((1024, 256), BF16),
-            pltpu.VMEM((2, 8, 128), F32),
             pltpu.VMEM((4, 16, 9, 8, 128), F32),
-            pltpu.VMEM((TAPS, 8, 128), F32),
+            pltpu.VMEM((64, 8, 128), F32),
+            pltpu.VMEM((128, 256), F32),
+            pltpu.VMEM((256, 128), F32),
             pltpu.VMEM(tile, F32),
             pltpu.VMEM((28, 10, 8, 128), BF16),
             pltpu.VMEM((28, 10, 8, 128), BF16),
@@ -548,10 +626,11 @@
             pltpu.VMEM((planes, chunk, 128), BF16),
             pltpu.VMEM((sizes[0], chunk, 128), BF16),
             pltpu.VMEM((planes, chunk, 128), BF16),
-            pltpu.VMEM((planes, small, 128), F32),
+            pltpu.VMEM((owners, small, 128), F32),
             pltpu.VMEM((planes, small, 128), F32),
             pltpu.VMEM((sizes[0], small, 128), F32),
-            pltpu.VMEM((planes, small, 128), F32),
+            pltpu.VMEM((owners, small, 128), F32),
+            dma((8,)),
             dma((9,)),
             dma((9,)),
             dma((9,)),
@@ -564,15 +643,29 @@
         ),
         name="ocean_block",
     )(
-        field.reshape(tile),
-        cotangent.reshape(tile),
-        land_mask,
-        kernel_taps,
-        norm_gain.reshape(1, 128),
-        norm_shift.reshape(1, 128),
-        up_weight,
-        down_weight,
+        *(
+            pltpu.with_memory_space_constraint(x, pltpu.HBM)
+            for x in (
+                field.reshape(tile),
+                cotangent.reshape(tile),
+                land_mask,
+                kernel_taps,
+                norm_gain.reshape(1, 128),
+                norm_shift.reshape(1, 128),
+                up_weight,
+                down_weight,
+            )
+        )
     )
+    out = pl.pallas_call(
+        write_out,
+        out_shape=results,
+        in_specs=[vmem] * 6,
+        out_specs=(hbm,) * 6,
+        scratch_shapes=[dma((6,))],
+        compiler_params=pltpu.CompilerParams(vmem_limit_bytes=8 * 1024 * 1024),
+        name="write_out",
+    )(*held)
     return (out[0].reshape(field.shape), out[1].reshape(field.shape)) + tuple(out[2:])
 
 

time: 69.8 us -> 56.7 us (0.81)
  local copies, waits for them, and re-layouts: 9.56 us -> 0 us
  Pallas kernels: 59.2 us -> 55.9 us
    unnamed x22 -> x0, local copies, waits for them, and re-layouts: 9.56 us -> none
    pallas_call x1 -> x2, Pallas kernels: 59.2 us -> 55.9 us  [the longest x1 55 us: shards(): pl.pallas_call(functools.partial(kernel, sizes), out_shape=results, in_sp...]
where the time goes in v2:
time: 56.7 us; the launch traced here: 56.6 us
  Pallas kernels  55.9 us (99%)
  between operations  0.64 us (1%)
    pallas_call x1, Pallas kernels, shards(): pl.pallas_call(functools.partial(kernel, sizes), out_shape=results, in_sp...  55 us

profile of v2, /device:TPU:1, one launch (start us, length us, event | category | flops | bytes accessed | tf_op | source)
XLA Modules:
  0.0 56.6 jit_solution(3420136278739736897)
XLA Ops:
  0.6 55.0 %ocean_block.1 = (bf16[16,8,8,128]{3,2,1,0:T(8,128)(2,1)S(1)}, bf16[16,8,8,128]{3,2,1,0:T(8,128)(2,1)S(1)}, f32[49,128]{1,0:T(8,128)S(1)}, f32[2,128]{1,0:T(2,12...) custom-call(bf16[16,8,8,128]{3,2,1,0:T(8,128)(2,1)} %bitcast.6, bf16[16,8,8,128]{3,2,1,0:T(8,128)(2,1)} %bitcast.7, ...), custom_call_target="tpu_custom_call" | custom-call | tf_op jit(solution)/shard_map/ocean_block/pallas_call | solution.py:595
  55.6 0.9 %write_out.1 = (bf16[16,8,8,128]{3,2,1,0:T(8,128)(2,1)}, bf16[16,8,8,128]{3,2,1,0:T(8,128)(2,1)}, f32[49,128]{1,0:T(8,128)}, f32[2,128]{1,0:T(2,128)}, f32[128,256]{1,0:T(8,128)}, /*index=5*/f32[256,128]{1,0:T(8,128)}) custom-call(bf16[16,8,8,128]{3,2,1,0:T(8,128)(2,1)S(1)} %get-tuple-element.18.refs_0_, ...), custom_call_target="tpu_custom_call" | custom-call | tf_op jit(solution)/shard_map/write_out/pallas_call | solution.py:660

commit v3 on v2

--- a/solution.py
+++ b/solution.py
@@ -58,6 +58,7 @@
         self.plane = self.lat * nens + self.ens
         self.planes = nlat * nens
         self.owners = min(8, self.planes)
+        self.relays = (nlat - 3, 1) if nlat == 8 else ()
         across, along = nlat // 2, nens // 2 * 2
         y = self.ens // 2 * 2 + lax.rem(self.lat, 2)
         core = lax.rem(self.ens, 2)
@@ -102,25 +103,102 @@
                 send(g.lat - 1, east, NORTH)
 
         else:
-            across = lax.rem(2 * g.nlon - 1 - g.lon - step, g.nlon)
 
             @pl.when(jnp.logical_not(g.north))
             def _(send=send, east=east):
                 send(g.lat + 1, east, SOUTH)
 
-            @pl.when(jnp.logical_and(g.north, across != g.lon))
-            def _(send=send, across=across):
-                send(g.lat, across, NORTH)
-
-            if cc != MIDDLE:
-
-                @pl.when(jnp.logical_and(g.north, across == g.lon))
-                def _(here=here, land_c=land_c):
-                    pltpu.make_async_copy(
-                        here,
-                        region(dst, DST_ROWS[NORTH], DST_COLS[land_c]),
-                        rsem.at[NORTH * 3 + land_c],
-                    ).start()
+
+def across(g, step):
+    return lax.rem(2 * g.nlon - 1 - g.lon - step, g.nlon)
+
+
+def fold_sends(g, here, dst, dst_row, count, cols, ssem, rsem, first_row):
+    for cc in (MIDDLE, EAST, WEST):
+        lon = across(g, cc - 1)
+        part = here.at[pl.ds(first_row, count), pl.ds(*cols[cc])]
+        land = dst.at[pl.ds(dst_row, count), pl.ds(*DST_COLS[2 - cc])]
+        arrived = rsem.at[NORTH * 3 + 2 - cc]
+
+        def go(part=part, land=land, arrived=arrived, lon=lon, cc=cc):
+            pltpu.make_async_remote_copy(
+                src_ref=part,
+                dst_ref=land,
+                send_sem=ssem(cc),
+                recv_sem=arrived,
+                device_id={"lon": lon, "lat": g.nlat - 1},
+                device_id_type=MESH,
+            ).start()
+
+        yield cc, lon, part, land, arrived, go
+
+
+def fold_start(g, src, dst, src_rows, src_cols, ssem, rsem, relay, rsems):
+    row, total = src_rows[NORTH]
+    own = total - 2 * len(g.relays)
+    for cc, lon, part, land, arrived, go in fold_sends(
+        g, src, dst, DST_ROWS[NORTH][0], own, src_cols, lambda cc: ssem.at[NORTH * 3 + cc], rsem, row
+    ):
+        if cc == MIDDLE:
+            for q, lat in enumerate(g.relays):
+                low, high = src_cols[WEST][0], src_cols[EAST][0] + 1
+                pltpu.make_async_remote_copy(
+                    src_ref=src.at[pl.ds(row + own + 2 * q, 2), pl.ds(low, high - low)],
+                    dst_ref=relay.at[pl.ds(0, 2), pl.ds(low, high - low)],
+                    send_sem=rsems.at[q],
+                    recv_sem=rsems.at[2],
+                    device_id={"lat": lat},
+                    device_id_type=MESH,
+                ).start()
+            go()
+        else:
+            pl.when(lon != g.lon)(go)
+
+            @pl.when(lon == g.lon)
+            def _(part=part, land=land, arrived=arrived):
+                pltpu.make_async_copy(part, land, arrived).start()
+
+
+def fold_pass_on(g, dst, src_cols, rsem, relay, rsems):
+    low, high = src_cols[WEST][0], src_cols[EAST][0] + 1
+    part = relay.at[pl.ds(0, 2), pl.ds(low, high - low)]
+    for q, lat in enumerate(g.relays):
+
+        @pl.when(g.lat == lat)
+        def _(q=q):
+            pltpu.make_async_copy(part, part, rsems.at[2]).wait()
+            row = DST_ROWS[NORTH][0] + 6 - 2 * len(g.relays) + 2 * q
+            for cc, lon, _, _, _, go in fold_sends(
+                g, relay, dst, row, 2, src_cols, lambda cc: rsems.at[3 + cc], rsem, 0
+            ):
+                go()
+
+
+def fold_wait_send(g, src, src_rows, src_cols, ssem, relay, rsems):
+    row, total = src_rows[NORTH]
+    own = total - 2 * len(g.relays)
+    low, high = src_cols[WEST][0], src_cols[EAST][0] + 1
+    whole = relay.at[pl.ds(0, 2), pl.ds(low, high - low)]
+
+    @pl.when(g.north)
+    def _():
+        for cc in range(3):
+            part = src.at[pl.ds(row, own), pl.ds(*src_cols[cc])]
+            wait = pltpu.make_async_copy(part, part, ssem.at[NORTH * 3 + cc]).wait
+            if cc == MIDDLE:
+                wait()
+            else:
+                pl.when(across(g, cc - 1) != g.lon)(wait)
+        for q in range(len(g.relays)):
+            pltpu.make_async_copy(whole, whole, rsems.at[q]).wait()
+
+    for lat in g.relays:
+
+        @pl.when(g.lat == lat)
+        def _():
+            for cc in range(3):
+                part = relay.at[pl.ds(0, 2), pl.ds(*src_cols[cc])]
+                pltpu.make_async_copy(part, part, rsems.at[3 + cc]).wait()
 
 
 def halo_wait_recv(g, dst, rsem, row):
@@ -143,11 +221,8 @@
             wait()
         elif rr == SOUTH:
             pl.when(g.lat > 0)(wait)
-        elif cc == MIDDLE:
-            wait()
         else:
-            across = lax.rem(2 * g.nlon - 1 - g.lon - (cc - 1), g.nlon)
-            pl.when(jnp.logical_or(jnp.logical_not(g.north), across != g.lon))(wait)
+            pl.when(jnp.logical_not(g.north))(wait)
 
 
 def plane_send(g, src_of, dst, ssem, rsem):
@@ -207,7 +282,7 @@
     field, cotangent, mask, taps, gain, shift, up, down,
     ext, sea, ep, kt, ups, mixed, normed, active, pregrad, mp, kacc, uacc, dacc, eg, egs, rb,
     pay1, ra1, zb1, gb1, pay2, ra2, zb2, gb2,
-    ins, fs, fr, bs, br, ar_s, ar_r,
+    relay_f, relay_b, ins, fs, fr, bs, br, ar_s, ar_r, rf, rb_s,
 ):
     g = Grid(*sizes)
     factor = 1.0 / math.sqrt(1024 * g.nlon * g.nlat * g.nens)
@@ -237,6 +312,15 @@
     for lon in g.lons:
         greet(lon=lon)
 
+    relay_here = jnp.int32(0)
+    for lat in g.relays:
+        relay_here = relay_here + (g.lat == lat).astype(jnp.int32)
+
+        @pl.when(g.north)
+        def _(lat=lat):
+            for step in (0, 1, -1):
+                greet(lat=lat, lon=across(g, step))
+
     east = lax.rem(g.lon + 1, g.nlon)
     west = lax.rem(g.lon + g.nlon - 1, g.nlon)
 
@@ -268,8 +352,13 @@
 
     count = g.planes + g.nlon - 2
     count = count + 2 * (g.lat > 0).astype(jnp.int32) + 2 * (g.lat < g.nlat - 1).astype(jnp.int32)
-    pl.semaphore_wait(barrier, count)
+    pl.semaphore_wait(barrier, count + 3 * relay_here)
     halo_start(g, ext, ext, FWD_ROWS, FWD_COLS, fs, fr, (CENTER, NORTH, SOUTH))
+
+    @pl.when(g.north)
+    def _():
+        fold_start(g, ext, ext, FWD_ROWS, FWD_COLS, fs, fr, relay_f, rf)
+
 
     loads["cotangent"].wait()
     for name in ("taps", "gain", "shift", "up", "down"):
@@ -293,6 +382,7 @@
         return carry
 
     halo_wait_recv(g, ext, fr, CENTER)
+    fold_pass_on(g, ext, FWD_COLS, fr, relay_f, rf)
     lax.fori_loop(REACH, 16 + REACH, widen_row, 0)
 
     halo_wait_recv(g, ext, fr, SOUTH)
@@ -434,6 +524,11 @@
         eg_halo(22 + 2 * m, 4 + m, 6)
     halo_start(g, egs, rb, BWD_ROWS, BWD_COLS, bs, br, (NORTH,))
 
+    @pl.when(g.north)
+    def _():
+        fold_start(g, egs, rb, BWD_ROWS, BWD_COLS, bs, br, relay_b, rb_s)
+
+
     chunk = 512 // g.planes
     per = 128 // chunk
     up_part = (uacc[...] + tdot(normed[640:1024, :], pregrad[640:1024, :])).astype(BF16)
@@ -463,6 +558,7 @@
     for m in range(3):
         eg_center(16 + 2 * m, 18 + 2 * m, 1 + m, 6)
     halo_start(g, egs, rb, BWD_ROWS, BWD_COLS, bs, br, (CENTER,))
+    fold_pass_on(g, rb, BWD_COLS, br, relay_b, rb_s)
 
     bulk_wait(ra1, g.planes - 1, ar_r.at[0])
     zb1[g.lon] = jnp.sum(ra1[...].astype(F32), 0).astype(BF16)
@@ -548,6 +644,8 @@
 
     halo_wait_send(g, ext, FWD_ROWS, FWD_COLS, fs)
     halo_wait_send(g, egs, BWD_ROWS, BWD_COLS, bs)
+    fold_wait_send(g, ext, FWD_ROWS, FWD_COLS, fs, relay_f, rf)
+    fold_wait_send(g, egs, BWD_ROWS, BWD_COLS, bs, relay_b, rb_s)
     bulk_wait(pay1, g.planes - 1, ar_s.at[0])
     bulk_wait(zb1, g.nlon - 1, ar_s.at[2])
     bulk_wait(gb1, g.planes - 1, ar_s.at[4])
@@ -630,11 +728,15 @@
             pltpu.VMEM((planes, small, 128), F32),
             pltpu.VMEM((sizes[0], small, 128), F32),
             pltpu.VMEM((owners, small, 128), F32),
+            pltpu.VMEM((2, 10, 8, 128), BF16),
+            pltpu.VMEM((2, 10, 8, 128), BF16),
             dma((8,)),
             dma((9,)),
             dma((9,)),
             dma((9,)),
             dma((9,)),
+            dma((6,)),
+            dma((6,)),
             dma((6,)),
             dma((6,)),
         ],

time: 56.7 us -> 54.1 us (0.954)
  Pallas kernels: 55.9 us -> 53.2 us
    pallas_call x1, Pallas kernels: 55 us -> 52.3 us  [shards(): pl.pallas_call(functools.partial(kernel, sizes), out_shape=results, in_sp...]
where the time goes in v3:
time: 54.1 us; the launch traced here: 53.9 us
  Pallas kernels  53.2 us (98%)
  between operations  0.64 us (1%)
    pallas_call x1, Pallas kernels, shards(): pl.pallas_call(functools.partial(kernel, sizes), out_shape=results, in_sp...  52.3 us

profile of v3, /device:TPU:1, one launch (start us, length us, event | category | flops | bytes accessed | tf_op | source)
XLA Modules:
  0.0 53.9 jit_solution(7772583623045596708)
XLA Ops:
  0.6 52.3 %ocean_block.1 = (bf16[16,8,8,128]{3,2,1,0:T(8,128)(2,1)S(1)}, bf16[16,8,8,128]{3,2,1,0:T(8,128)(2,1)S(1)}, f32[49,128]{1,0:T(8,128)S(1)}, f32[2,128]{1,0:T(2,12...) custom-call(bf16[16,8,8,128]{3,2,1,0:T(8,128)(2,1)} %bitcast.6, bf16[16,8,8,128]{3,2,1,0:T(8,128)(2,1)} %bitcast.7, ...), custom_call_target="tpu_custom_call" | custom-call | tf_op jit(solution)/shard_map/ocean_block/pallas_call | solution.py:693
  53.0 0.9 %write_out.1 = (bf16[16,8,8,128]{3,2,1,0:T(8,128)(2,1)}, bf16[16,8,8,128]{3,2,1,0:T(8,128)(2,1)}, f32[49,128]{1,0:T(8,128)}, f32[2,128]{1,0:T(2,128)}, f32[128,256]{1,0:T(8,128)}, /*index=5*/f32[256,128]{1,0:T(8,128)}) custom-call(bf16[16,8,8,128]{3,2,1,0:T(8,128)(2,1)S(1)} %get-tuple-element.18.refs_0_, ...), custom_call_target="tpu_custom_call" | custom-call | tf_op jit(solution)/shard_map/write_out/pallas_call | solution.py:762

commit v4 on v3

--- a/solution.py
+++ b/solution.py
@@ -57,8 +57,17 @@
         self.north = self.lat == nlat - 1
         self.plane = self.lat * nens + self.ens
         self.planes = nlat * nens
-        self.owners = min(8, self.planes)
-        self.relays = (nlat - 3, 1) if nlat == 8 else ()
+        if nlat == 8 and nens == 4:
+            self.owner_at = [(lat, ens) for lat in (0, 2, 4, 6) for ens in (0, 2)]
+            self.owner = (lax.rem(self.lat, 2) + lax.rem(self.ens, 2)) == 0
+            self.owned = self.lat // 2 * 2 + self.ens // 2
+        else:
+            self.owner_at = [(p // nens, p % nens) for p in range(min(8, self.planes))]
+            self.owner = self.plane < len(self.owner_at)
+            self.owned = self.plane
+        self.owners = len(self.owner_at)
+        self.relays = ((nlat - 3, 2), (1, 2)) if nlat == 8 else ()
+        self.relayed = sum(rows for _, rows in self.relays)
         across, along = nlat // 2, nens // 2 * 2
         y = self.ens // 2 * 2 + lax.rem(self.lat, 2)
         core = lax.rem(self.ens, 2)
@@ -133,23 +142,30 @@
         yield cc, lon, part, land, arrived, go
 
 
+def relay_part(g, relay, src_cols, rows):
+    low, high = src_cols[WEST][0], src_cols[EAST][0] + 1
+    return relay.at[pl.ds(0, rows), pl.ds(low, high - low)]
+
+
 def fold_start(g, src, dst, src_rows, src_cols, ssem, rsem, relay, rsems):
     row, total = src_rows[NORTH]
-    own = total - 2 * len(g.relays)
+    low, high = src_cols[WEST][0], src_cols[EAST][0] + 1
+    own = total - g.relayed
+    first = row + own
+    for q, (lat, rows) in enumerate(g.relays):
+        pltpu.make_async_remote_copy(
+            src_ref=src.at[pl.ds(first, rows), pl.ds(low, high - low)],
+            dst_ref=relay_part(g, relay, src_cols, rows),
+            send_sem=rsems.at[q],
+            recv_sem=rsems.at[3],
+            device_id={"lat": lat},
+            device_id_type=MESH,
+        ).start()
+        first += rows
     for cc, lon, part, land, arrived, go in fold_sends(
         g, src, dst, DST_ROWS[NORTH][0], own, src_cols, lambda cc: ssem.at[NORTH * 3 + cc], rsem, row
     ):
         if cc == MIDDLE:
-            for q, lat in enumerate(g.relays):
-                low, high = src_cols[WEST][0], src_cols[EAST][0] + 1
-                pltpu.make_async_remote_copy(
-                    src_ref=src.at[pl.ds(row + own + 2 * q, 2), pl.ds(low, high - low)],
-                    dst_ref=relay.at[pl.ds(0, 2), pl.ds(low, high - low)],
-                    send_sem=rsems.at[q],
-                    recv_sem=rsems.at[2],
-                    device_id={"lat": lat},
-                    device_id_type=MESH,
-                ).start()
             go()
         else:
             pl.when(lon != g.lon)(go)
@@ -160,25 +176,24 @@
 
 
 def fold_pass_on(g, dst, src_cols, rsem, relay, rsems):
-    low, high = src_cols[WEST][0], src_cols[EAST][0] + 1
-    part = relay.at[pl.ds(0, 2), pl.ds(low, high - low)]
-    for q, lat in enumerate(g.relays):
+    first = DST_ROWS[NORTH][0] + DST_ROWS[NORTH][1] - g.relayed
+    for lat, rows in g.relays:
 
         @pl.when(g.lat == lat)
-        def _(q=q):
-            pltpu.make_async_copy(part, part, rsems.at[2]).wait()
-            row = DST_ROWS[NORTH][0] + 6 - 2 * len(g.relays) + 2 * q
+        def _(first=first, rows=rows):
+            part = relay_part(g, relay, src_cols, rows)
+            pltpu.make_async_copy(part, part, rsems.at[3]).wait()
             for cc, lon, _, _, _, go in fold_sends(
-                g, relay, dst, row, 2, src_cols, lambda cc: rsems.at[3 + cc], rsem, 0
+                g, relay, dst, first, rows, src_cols, lambda cc: rsems.at[4 + cc], rsem, 0
             ):
                 go()
 
+        first += rows
+
 
 def fold_wait_send(g, src, src_rows, src_cols, ssem, relay, rsems):
     row, total = src_rows[NORTH]
-    own = total - 2 * len(g.relays)
-    low, high = src_cols[WEST][0], src_cols[EAST][0] + 1
-    whole = relay.at[pl.ds(0, 2), pl.ds(low, high - low)]
+    own = total - g.relayed
 
     @pl.when(g.north)
     def _():
@@ -189,16 +204,17 @@
                 wait()
             else:
                 pl.when(across(g, cc - 1) != g.lon)(wait)
-        for q in range(len(g.relays)):
+        for q, (_, rows) in enumerate(g.relays):
+            whole = relay_part(g, relay, src_cols, rows)
             pltpu.make_async_copy(whole, whole, rsems.at[q]).wait()
 
-    for lat in g.relays:
+    for lat, rows in g.relays:
 
         @pl.when(g.lat == lat)
-        def _():
+        def _(rows=rows):
             for cc in range(3):
-                part = relay.at[pl.ds(0, 2), pl.ds(*src_cols[cc])]
-                pltpu.make_async_copy(part, part, rsems.at[3 + cc]).wait()
+                part = relay.at[pl.ds(0, rows), pl.ds(*src_cols[cc])]
+                pltpu.make_async_copy(part, part, rsems.at[4 + cc]).wait()
 
 
 def halo_wait_recv(g, dst, rsem, row):
@@ -225,11 +241,12 @@
             pl.when(jnp.logical_not(g.north))(wait)
 
 
-def plane_send(g, src_of, dst, ssem, rsem):
+def plane_send(g, src_of, dst, ssem, rsem, slot=None):
+    slot = g.plane if slot is None else slot
     for lat, ens in g.peers:
         pltpu.make_async_remote_copy(
             src_ref=src_of(lat * g.nens + ens),
-            dst_ref=dst.at[g.plane],
+            dst_ref=dst.at[slot],
             send_sem=ssem,
             recv_sem=rsem,
             device_id={"lat": lat, "ens": ens},
@@ -238,16 +255,16 @@
 
 
 def owner_send(g, src, dst, ssem, rsem):
-    for o in range(g.owners):
-
-        @pl.when(g.plane != o)
-        def _(o=o):
+    for o, (lat, ens) in enumerate(g.owner_at):
+
+        @pl.when(g.plane != lat * g.nens + ens)
+        def _(o=o, lat=lat, ens=ens):
             pltpu.make_async_remote_copy(
                 src_ref=src.at[o],
                 dst_ref=dst.at[g.plane],
                 send_sem=ssem,
                 recv_sem=rsem,
-                device_id={"lat": o // g.nens, "ens": o % g.nens},
+                device_id={"lat": lat, "ens": ens},
                 device_id_type=MESH,
             ).start()
 
@@ -286,7 +303,7 @@
 ):
     g = Grid(*sizes)
     factor = 1.0 / math.sqrt(1024 * g.nlon * g.nlat * g.nens)
-    owner = g.plane < g.owners
+    owner = g.owner
 
     loads = {}
     for k, (name, src, dst) in enumerate(
@@ -312,15 +329,6 @@
     for lon in g.lons:
         greet(lon=lon)
 
-    relay_here = jnp.int32(0)
-    for lat in g.relays:
-        relay_here = relay_here + (g.lat == lat).astype(jnp.int32)
-
-        @pl.when(g.north)
-        def _(lat=lat):
-            for step in (0, 1, -1):
-                greet(lat=lat, lon=across(g, step))
-
     east = lax.rem(g.lon + 1, g.nlon)
     west = lax.rem(g.lon + g.nlon - 1, g.nlon)
 
@@ -352,12 +360,13 @@
 
     count = g.planes + g.nlon - 2
     count = count + 2 * (g.lat > 0).astype(jnp.int32) + 2 * (g.lat < g.nlat - 1).astype(jnp.int32)
-    pl.semaphore_wait(barrier, count + 3 * relay_here)
+    pl.semaphore_wait(barrier, count)
+
+    @pl.when(g.north)
+    def _():
+        fold_start(g, ext, ext, FWD_ROWS, FWD_COLS, fs, fr, relay_f, rf)
+
     halo_start(g, ext, ext, FWD_ROWS, FWD_COLS, fs, fr, (CENTER, NORTH, SOUTH))
-
-    @pl.when(g.north)
-    def _():
-        fold_start(g, ext, ext, FWD_ROWS, FWD_COLS, fs, fr, relay_f, rf)
 
 
     loads["cotangent"].wait()
@@ -381,17 +390,9 @@
             ep[k + 1, r, 0:9] = moved
         return carry
 
+    fold_pass_on(g, ext, FWD_COLS, fr, relay_f, rf)
     halo_wait_recv(g, ext, fr, CENTER)
-    fold_pass_on(g, ext, FWD_COLS, fr, relay_f, rf)
     lax.fori_loop(REACH, 16 + REACH, widen_row, 0)
-
-    halo_wait_recv(g, ext, fr, SOUTH)
-
-    @pl.when(g.lat == 0)
-    def _():
-        ext[0:REACH] = jnp.zeros((REACH, 10, 8, 128), BF16)
-
-    lax.fori_loop(0, REACH, widen_row, 0)
 
     def conv_row(r, carry):
         total = jnp.zeros((8, 8, 128), F32)
@@ -458,8 +459,16 @@
                 kacc[i * KERNEL + j] += jnp.sum(grad * ep[ph, r + 2 * i, skip : skip + 8], 0)
         return carry
 
-    group(0, 5)
-    group(5, 5)
+    group(6, 4)
+    halo_wait_recv(g, ext, fr, SOUTH)
+
+    @pl.when(g.lat == 0)
+    def _():
+        ext[0:REACH] = jnp.zeros((REACH, 10, 8, 128), BF16)
+
+    lax.fori_loop(0, REACH, widen_row, 0)
+
+    group(0, 6)
     lax.fori_loop(0, 10, tap_row, 0)
     lax.fori_loop(0, 10, spread_row, 0)
     uacc[...] = tdot(normed[0:640, :], pregrad[0:640, :])
@@ -541,11 +550,11 @@
 
     lax.fori_loop(10, 16, tap_row, 0)
     small = 64 // g.owners
-    pay2[...] = jnp.sum(kacc[...], 1).reshape(g.owners, small, 128)
+    pay2[...] = jnp.sum(kacc[...], 1).reshape(g.owners, small, 128).astype(BF16)
 
     @pl.when(owner)
     def _():
-        ra2[g.plane] = pay2[g.plane]
+        ra2[g.plane] = pay2[g.owned]
 
     owner_send(g, pay2, ra2, ar_s.at[1], ar_r.at[1])
 
@@ -567,8 +576,18 @@
     @pl.when(owner)
     def _():
         bulk_wait(ra2, g.planes - 1, ar_r.at[1])
-        zb2[g.lon] = jnp.sum(ra2[...], 0)
+        zb2[g.lon] = jnp.sum(ra2[...].astype(F32), 0).astype(BF16)
         lon_send(g, zb2, ar_s.at[3], ar_r.at[3])
+
+    bulk_wait(zb1, g.nlon - 1, ar_r.at[2])
+    gb1[g.plane] = jnp.sum(zb1[...].astype(F32), 0).astype(BF16)
+    plane_send(g, lambda peer: gb1.at[g.plane], gb1, ar_s.at[4], ar_r.at[4])
+
+    @pl.when(owner)
+    def _():
+        bulk_wait(zb2, g.nlon - 1, ar_r.at[3])
+        gb2[g.owned] = jnp.sum(zb2[...].astype(F32), 0).astype(BF16)
+        plane_send(g, lambda peer: gb2.at[g.owned], gb2, ar_s.at[5], ar_r.at[5], g.owned)
 
     halo_wait_recv(g, rb, br, CENTER)
 
@@ -615,16 +634,6 @@
 
     lax.fori_loop(0, 16, last_row, 0, unroll=2)
 
-    bulk_wait(zb1, g.nlon - 1, ar_r.at[2])
-    gb1[g.plane] = jnp.sum(zb1[...].astype(F32), 0).astype(BF16)
-    plane_send(g, lambda peer: gb1.at[g.plane], gb1, ar_s.at[4], ar_r.at[4])
-
-    @pl.when(owner)
-    def _():
-        bulk_wait(zb2, g.nlon - 1, ar_r.at[3])
-        gb2[g.plane] = jnp.sum(zb2[...], 0)
-        plane_send(g, lambda peer: gb2.at[g.plane], gb2, ar_s.at[5], ar_r.at[5])
-
     bulk_wait(gb1, g.planes - 1, ar_r.at[4])
     up_grad[:, 0:128] = gb1[0:per].astype(F32).reshape(128, 128) * factor
     up_grad[:, 128:256] = gb1[per : 2 * per].astype(F32).reshape(128, 128) * factor
@@ -638,7 +647,7 @@
     def _():
         bulk_wait(gb2, g.owners, ar_r.at[5])
 
-    small_sums = gb2[...].reshape(64, 128) * factor
+    small_sums = gb2[...].astype(F32).reshape(64, 128) * factor
     kernel_grad[...] = small_sums[0:TAPS]
     norm_grad[...] = small_sums[TAPS : TAPS + 2]
 
@@ -724,10 +733,10 @@
             pltpu.VMEM((planes, chunk, 128), BF16),
             pltpu.VMEM((sizes[0], chunk, 128), BF16),
             pltpu.VMEM((planes, chunk, 128), BF16),
-            pltpu.VMEM((owners, small, 128), F32),
-            pltpu.VMEM((planes, small, 128), F32),
-            pltpu.VMEM((sizes[0], small, 128), F32),
-            pltpu.VMEM((owners, small, 128), F32),
+            pltpu.VMEM((owners, small, 128), BF16),
+            pltpu.VMEM((planes, small, 128), BF16),
+            pltpu.VMEM((sizes[0], small, 128), BF16),
+            pltpu.VMEM((owners, small, 128), BF16),
             pltpu.VMEM((2, 10, 8, 128), BF16),
             pltpu.VMEM((2, 10, 8, 128), BF16),
             dma((8,)),
@@ -737,8 +746,8 @@
             dma((9,)),
             dma((6,)),
             dma((6,)),
-            dma((6,)),
-            dma((6,)),
+            dma((7,)),
+            dma((7,)),
         ],
         compiler_params=pltpu.CompilerParams(
             collective_id=0, has_side_effects=True, vmem_limit_bytes=48 * 1024 * 1024

time: 54.1 us -> 52.1 us (0.963)
  Pallas kernels: 53.2 us -> 51.3 us
    pallas_call x1, Pallas kernels: 52.3 us -> 50.4 us  [shards(): pl.pallas_call(functools.partial(kernel, sizes), out_shape=results, in_sp...]
where the time goes in v4:
time: 52.1 us; the launch traced here: 51.9 us
  Pallas kernels  51.3 us (98%)
  between operations  0.64 us (1%)
    pallas_call x1, Pallas kernels, shards(): pl.pallas_call(functools.partial(kernel, sizes), out_shape=results, in_sp...  50.4 us

profile of v4, /device:TPU:1, one launch (start us, length us, event | category | flops | bytes accessed | tf_op | source)
XLA Modules:
  0.0 51.9 jit_solution(833959329476738534)
XLA Ops:
  0.6 50.4 %ocean_block.1 = (bf16[16,8,8,128]{3,2,1,0:T(8,128)(2,1)S(1)}, bf16[16,8,8,128]{3,2,1,0:T(8,128)(2,1)S(1)}, f32[49,128]{1,0:T(8,128)S(1)}, f32[2,128]{1,0:T(2,12...) custom-call(bf16[16,8,8,128]{3,2,1,0:T(8,128)(2,1)} %bitcast.6, bf16[16,8,8,128]{3,2,1,0:T(8,128)(2,1)} %bitcast.7, ...), custom_call_target="tpu_custom_call" | custom-call | tf_op jit(solution)/shard_map/ocean_block/pallas_call | solution.py:702
  51.0 0.9 %write_out.1 = (bf16[16,8,8,128]{3,2,1,0:T(8,128)(2,1)}, bf16[16,8,8,128]{3,2,1,0:T(8,128)(2,1)}, f32[49,128]{1,0:T(8,128)}, f32[2,128]{1,0:T(2,128)}, f32[128,256]{1,0:T(8,128)}, /*index=5*/f32[256,128]{1,0:T(8,128)}) custom-call(bf16[16,8,8,128]{3,2,1,0:T(8,128)(2,1)S(1)} %get-tuple-element.18.refs_0_, ...), custom_call_target="tpu_custom_call" | custom-call | tf_op jit(solution)/shard_map/write_out/pallas_call | solution.py:771

commit v5 on v4

--- a/solution.py
+++ b/solution.py
@@ -71,6 +71,20 @@
         across, along = nlat // 2, nens // 2 * 2
         y = self.ens // 2 * 2 + lax.rem(self.lat, 2)
         core = lax.rem(self.ens, 2)
+        hop = lambda d: {"lon": lax.rem(self.lon + d + nlon, nlon)}
+        x, low, high = self.lat // 2, lax.rem(self.lat, 2), self.ens // 2
+        self.first = [hop(d) for d in (1, -1, 2, -2)]
+        self.lon_rounds = [[hop(d), hop(-d)] for d in (2, 4) if 2 * d <= nlon]
+        twin = {"ens": high * 2 + (1 - core)}
+        beside = {"lat": x * 2 + (1 - low)}
+        self.plane_rounds = [[twin], [beside]]
+        if along == 4:
+            self.plane_rounds.insert(1, [{"ens": (1 - high) * 2 + core}])
+        if across == 4:
+            ring = [{"lat": lax.rem(x + d, 4) * 2 + low} for d in (1, 3)]
+            self.plane_rounds += [ring, ring]
+        for near in self.plane_rounds[: 3 if along == 4 else 2] + self.plane_rounds[3:4]:
+            self.first += near
         xs = [lax.rem(self.lat // 2 + d, across) for d in range(across)]
         ys = [lax.rem(y + d, along) for d in range(along)]
         steps = [(dx, dy, dc) for dx in range(across) for dy in range(along) for dc in range(2)][1:]
@@ -147,11 +161,9 @@
     return relay.at[pl.ds(0, rows), pl.ds(low, high - low)]
 
 
-def fold_start(g, src, dst, src_rows, src_cols, ssem, rsem, relay, rsems):
-    row, total = src_rows[NORTH]
+def relay_send(g, src, src_rows, src_cols, relay, rsems):
     low, high = src_cols[WEST][0], src_cols[EAST][0] + 1
-    own = total - g.relayed
-    first = row + own
+    first = sum(src_rows[NORTH]) - g.relayed
     for q, (lat, rows) in enumerate(g.relays):
         pltpu.make_async_remote_copy(
             src_ref=src.at[pl.ds(first, rows), pl.ds(low, high - low)],
@@ -162,8 +174,20 @@
             device_id_type=MESH,
         ).start()
         first += rows
+
+
+def fold_own(g, src, dst, src_rows, src_cols, ssem, rsem):
+    row, total = src_rows[NORTH]
     for cc, lon, part, land, arrived, go in fold_sends(
-        g, src, dst, DST_ROWS[NORTH][0], own, src_cols, lambda cc: ssem.at[NORTH * 3 + cc], rsem, row
+        g,
+        src,
+        dst,
+        DST_ROWS[NORTH][0],
+        total - g.relayed,
+        src_cols,
+        lambda cc: ssem.at[NORTH * 3 + cc],
+        rsem,
+        row,
     ):
         if cc == MIDDLE:
             go()
@@ -299,7 +323,7 @@
     field, cotangent, mask, taps, gain, shift, up, down,
     ext, sea, ep, kt, ups, mixed, normed, active, pregrad, mp, kacc, uacc, dacc, eg, egs, rb,
     pay1, ra1, zb1, gb1, pay2, ra2, zb2, gb2,
-    relay_f, relay_b, ins, fs, fr, bs, br, ar_s, ar_r, rf, rb_s,
+    relay_f, relay_b, ins, fs, fr, bs, br, ar_s, ar_r, rf, rb_s, lon_sem, plane_sem,
 ):
     g = Grid(*sizes)
     factor = 1.0 / math.sqrt(1024 * g.nlon * g.nlat * g.nens)
@@ -326,24 +350,36 @@
     def greet(**where):
         pl.semaphore_signal(barrier, inc=1, device_id=where, device_id_type=MESH)
 
-    for lon in g.lons:
-        greet(lon=lon)
-
+    for where in g.first:
+        greet(**where)
     east = lax.rem(g.lon + 1, g.nlon)
     west = lax.rem(g.lon + g.nlon - 1, g.nlon)
 
     @pl.when(g.lat > 0)
     def _():
-        greet(lat=g.lat - 1, lon=east)
-        greet(lat=g.lat - 1, lon=west)
+        for lon in (east, west, g.lon):
+            greet(lat=g.lat - 1, lon=lon)
 
     @pl.when(g.lat < g.nlat - 1)
     def _():
-        greet(lat=g.lat + 1, lon=east)
-        greet(lat=g.lat + 1, lon=west)
-
-    for lat, ens in g.peers:
-        greet(lat=lat, ens=ens)
+        for lon in (east, west, g.lon):
+            greet(lat=g.lat + 1, lon=lon)
+
+    relay = jnp.int32(0)
+    for lat, _ in g.relays:
+        relay = relay + (g.lat == lat).astype(jnp.int32)
+
+        @pl.when(g.north)
+        def _(lat=lat):
+            for where in g.first[:4]:
+                greet(lat=lat, **where)
+
+    def tell(rounds, sem, k):
+        for where in rounds[k]:
+            pl.semaphore_signal(sem.at[k], inc=1, device_id=where, device_id_type=MESH)
+
+    def hear(rounds, sem, k):
+        pl.semaphore_wait(sem.at[k], len(rounds[k]))
 
     eye = (
         lax.broadcasted_iota(jnp.int32, (64, 64), 0) == lax.broadcasted_iota(jnp.int32, (64, 64), 1)
@@ -358,13 +394,14 @@
         sea[r] = wide
         ext[r + REACH, 1:9] = (field[r].astype(F32) * wide).astype(BF16)
 
-    count = g.planes + g.nlon - 2
-    count = count + 2 * (g.lat > 0).astype(jnp.int32) + 2 * (g.lat < g.nlat - 1).astype(jnp.int32)
-    pl.semaphore_wait(barrier, count)
+    sides = (g.lat > 0).astype(jnp.int32) + (g.lat < g.nlat - 1).astype(jnp.int32)
+    pl.semaphore_wait(barrier, len(g.first) + 3 * sides + 4 * relay)
+    tell(g.lon_rounds, lon_sem, 0)
+    tell(g.plane_rounds, plane_sem, 0)
 
     @pl.when(g.north)
     def _():
-        fold_start(g, ext, ext, FWD_ROWS, FWD_COLS, fs, fr, relay_f, rf)
+        relay_send(g, ext, FWD_ROWS, FWD_COLS, relay_f, rf)
 
     halo_start(g, ext, ext, FWD_ROWS, FWD_COLS, fs, fr, (CENTER, NORTH, SOUTH))
 
@@ -390,7 +427,10 @@
             ep[k + 1, r, 0:9] = moved
         return carry
 
-    fold_pass_on(g, ext, FWD_COLS, fr, relay_f, rf)
+    hear(g.lon_rounds, lon_sem, 0)
+    tell(g.lon_rounds, lon_sem, 1)
+    hear(g.plane_rounds, plane_sem, 0)
+    tell(g.plane_rounds, plane_sem, 1)
     halo_wait_recv(g, ext, fr, CENTER)
     lax.fori_loop(REACH, 16 + REACH, widen_row, 0)
 
@@ -407,8 +447,23 @@
     gain_row = gain[...]
     shift_row = shift[...]
 
-    def group(first, many):
-        lax.fori_loop(first, first + many, conv_row, 0)
+    def conv_pair(start, taps_i, more):
+        def one(r, carry):
+            cells = pl.ds(pl.multiple_of(r * 64, 64), 64)
+            total = mixed[cells, :].reshape(8, 8, 128) if more else jnp.zeros((8, 8, 128), F32)
+            for i in taps_i:
+                for j in range(KERNEL):
+                    off = 2 + 2 * j
+                    ph, skip = (off % 8) // 2, off // 8
+                    total = total + kt[i * KERNEL + j][None] * ep[ph, r + 2 * i, skip : skip + 8]
+            mixed[cells, :] = total.reshape(64, 128)
+            return carry
+
+        lax.fori_loop(start, start + 2, one, 0)
+
+    def group(first, many, conv=True):
+        if conv:
+            lax.fori_loop(first, first + many, conv_row, 0)
         cells = slice(64 * first, 64 * (first + many))
         rows = slice(first, first + many)
         x = mixed[cells, :]
@@ -459,7 +514,22 @@
                 kacc[i * KERNEL + j] += jnp.sum(grad * ep[ph, r + 2 * i, skip : skip + 8], 0)
         return carry
 
+    hear(g.plane_rounds, plane_sem, 1)
+    tell(g.plane_rounds, plane_sem, 2)
+    crossing = jnp.logical_or(g.north, relay > 0)
+
+    @pl.when(crossing)
+    def _():
+        hear(g.lon_rounds, lon_sem, 1)
+
+    @pl.when(g.north)
+    def _():
+        fold_own(g, ext, ext, FWD_ROWS, FWD_COLS, fs, fr)
+
+    fold_pass_on(g, ext, FWD_COLS, fr, relay_f, rf)
     group(6, 4)
+    hear(g.plane_rounds, plane_sem, 2)
+    tell(g.plane_rounds, plane_sem, 3)
     halo_wait_recv(g, ext, fr, SOUTH)
 
     @pl.when(g.lat == 0)
@@ -468,11 +538,15 @@
 
     lax.fori_loop(0, REACH, widen_row, 0)
 
+    hear(g.plane_rounds, plane_sem, 3)
+    tell(g.plane_rounds, plane_sem, 4)
     group(0, 6)
     lax.fori_loop(0, 10, tap_row, 0)
     lax.fori_loop(0, 10, spread_row, 0)
     uacc[...] = tdot(normed[0:640, :], pregrad[0:640, :])
     dacc[...] = tdot(active[0:640, :], ups[0:640, :])
+    for m in range(3):
+        conv_pair(10 + 2 * m, range(6 - m), False)
     halo_wait_recv(g, ext, fr, NORTH)
 
     flip = (
@@ -495,9 +569,9 @@
             for s, moved in enumerate(phases_of(turned)):
                 ep[s + 1, r, 0:9] = moved
 
-    group(10, 6)
-    lax.fori_loop(10, 16, spread_row, 0)
-
+    for m in range(3):
+        conv_pair(10 + 2 * m, range(6 - m, KERNEL), True)
+    group(10, 6, False)
     def eg_row(p, first, last):
         lo = jnp.zeros((9, 8, 128), F32)
         hi = jnp.zeros((9, 8, 128), F32)
@@ -529,15 +603,6 @@
 
         lax.fori_loop(start, stop, one, 0)
 
-    for m in range(3):
-        eg_halo(22 + 2 * m, 4 + m, 6)
-    halo_start(g, egs, rb, BWD_ROWS, BWD_COLS, bs, br, (NORTH,))
-
-    @pl.when(g.north)
-    def _():
-        fold_start(g, egs, rb, BWD_ROWS, BWD_COLS, bs, br, relay_b, rb_s)
-
-
     chunk = 512 // g.planes
     per = 128 // chunk
     up_part = (uacc[...] + tdot(normed[640:1024, :], pregrad[640:1024, :])).astype(BF16)
@@ -546,6 +611,7 @@
     down_part = (dacc[...] + tdot(active[640:1024, :], ups[640:1024, :])).astype(BF16)
     pay1[2 * per : 4 * per] = down_part.reshape(2 * per, chunk, 128)
     ra1[g.plane] = pay1[g.plane]
+    hear(g.plane_rounds, plane_sem, 4)
     plane_send(g, lambda peer: pay1.at[peer], ra1, ar_s.at[0], ar_r.at[0])
 
     lax.fori_loop(10, 16, tap_row, 0)
@@ -557,6 +623,18 @@
         ra2[g.plane] = pay2[g.owned]
 
     owner_send(g, pay2, ra2, ar_s.at[1], ar_r.at[1])
+
+    lax.fori_loop(10, 16, spread_row, 0)
+
+    for m in range(3):
+        eg_halo(22 + 2 * m, 4 + m, 6)
+    halo_start(g, egs, rb, BWD_ROWS, BWD_COLS, bs, br, (NORTH,))
+
+    @pl.when(g.north)
+    def _():
+        relay_send(g, egs, BWD_ROWS, BWD_COLS, relay_b, rb_s)
+        fold_own(g, egs, rb, BWD_ROWS, BWD_COLS, bs, br)
+
 
     for m in range(3):
         eg_halo(2 * m, 0, m)
@@ -568,6 +646,10 @@
         eg_center(16 + 2 * m, 18 + 2 * m, 1 + m, 6)
     halo_start(g, egs, rb, BWD_ROWS, BWD_COLS, bs, br, (CENTER,))
     fold_pass_on(g, rb, BWD_COLS, br, relay_b, rb_s)
+
+    @pl.when(jnp.logical_not(crossing))
+    def _():
+        hear(g.lon_rounds, lon_sem, 1)
 
     bulk_wait(ra1, g.planes - 1, ar_r.at[0])
     zb1[g.lon] = jnp.sum(ra1[...].astype(F32), 0).astype(BF16)
@@ -748,6 +830,8 @@
             dma((6,)),
             dma((7,)),
             dma((7,)),
+            pltpu.SemaphoreType.REGULAR((2,)),
+            pltpu.SemaphoreType.REGULAR((5,)),
         ],
         compiler_params=pltpu.CompilerParams(
             collective_id=0, has_side_effects=True, vmem_limit_bytes=48 * 1024 * 1024

time: 52.1 us -> 49.8 us (0.956)
  Pallas kernels: 51.3 us -> 49 us
    pallas_call x1, Pallas kernels: 50.4 us -> 48.1 us  [shards(): pl.pallas_call(functools.partial(kernel, sizes), out_shape=results, in_sp...]
where the time goes in v5:
time: 49.8 us; the launch traced here: 49.6 us
  Pallas kernels  49 us (98%)
  between operations  0.64 us (1%)
    pallas_call x1, Pallas kernels, shards(): pl.pallas_call(functools.partial(kernel, sizes), out_shape=results, in_sp...  48.1 us

profile of v5, /device:TPU:1, one launch (start us, length us, event | category | flops | bytes accessed | tf_op | source)
XLA Modules:
  0.0 49.6 jit_solution(1682216119940094430)
XLA Ops:
  0.6 48.1 %ocean_block.1 = (bf16[16,8,8,128]{3,2,1,0:T(8,128)(2,1)S(1)}, bf16[16,8,8,128]{3,2,1,0:T(8,128)(2,1)S(1)}, f32[49,128]{1,0:T(8,128)S(1)}, f32[2,128]{1,0:T(2,12...) custom-call(bf16[16,8,8,128]{3,2,1,0:T(8,128)(2,1)} %bitcast.6, bf16[16,8,8,128]{3,2,1,0:T(8,128)(2,1)} %bitcast.7, ...), custom_call_target="tpu_custom_call" | custom-call | tf_op jit(solution)/shard_map/ocean_block/pallas_call | solution.py:784
  48.7 0.9 %write_out.1 = (bf16[16,8,8,128]{3,2,1,0:T(8,128)(2,1)}, bf16[16,8,8,128]{3,2,1,0:T(8,128)(2,1)}, f32[49,128]{1,0:T(8,128)}, f32[2,128]{1,0:T(2,128)}, f32[128,256]{1,0:T(8,128)}, /*index=5*/f32[256,128]{1,0:T(8,128)}) custom-call(bf16[16,8,8,128]{3,2,1,0:T(8,128)(2,1)S(1)} %get-tuple-element.18.refs_0_, ...), custom_call_target="tpu_custom_call" | custom-call | tf_op jit(solution)/shard_map/write_out/pallas_call | solution.py:855
